TPU v7x, 512 devices: a whole 4x8x8 slice. The times are simulated.
512 devices in a mesh: prow: 16 (over y, core), pcol: 32 (over z, x).
Axes of the slice: x: 4, y: 8, z: 8, core: 2. Of those that a mesh axis runs over, the one named last changes fastest.
Arguments:
- matrix: bfloat16 [2, 16, 512, 2, 32, 512], P(None, 'prow', None, None, 'pcol'), may hold values from -6 to 6
- pivots: int32 [2, 512], replicated, may hold values from 0 to 16383, as said below
- lower_inverse: bfloat16 [2, 512, 512], replicated, as said below
- upper_inverse: bfloat16 [2, 512, 512], replicated, as said below
Outputs:
- factored: bfloat16 [2, 16, 512, 2, 32, 512], P(None, 'prow', None, None, 'pcol')
Inputs may be any that keep to these rules, and one draw needn't show every extreme that they name: Each row of pivots holds 512 distinct row indices; those of panel k are k * 512 or more. lower_inverse[k] is unit lower triangular. upper_inverse[k] is upper triangular with a positive diagonal.
All inputs are finite; a program needn't handle non-finite values.
Results may differ from a plain program's by a relative error of at most 0.0084.
Values may be sent and summed in bfloat16 or wider, within the bound.
A program may use at most 64 MiB of HBM per device.

v0:
```python
import jax
import jax.numpy as jnp
from jax import lax
from jax.sharding import PartitionSpec as P

PANELS = 2


def from_root(value, axis, root):
    mine = lax.axis_index(axis) == root
    return lax.psum(jnp.where(mine, value, jnp.zeros_like(value)), axis)


def pairing(sources, first_row, panel_width):
    top_ids = first_row + jnp.arange(panel_width, dtype=jnp.int32)
    chosen = jnp.any(sources[None, :] == top_ids[:, None], axis=1)
    leftover = jnp.logical_not(chosen)
    left_rank = jnp.cumsum(leftover.astype(jnp.int32)) - 1
    vacated = sources >= first_row + panel_width
    vac_rank = jnp.cumsum(vacated.astype(jnp.int32)) - 1
    match_table = leftover[None, :] & (left_rank[None, :] == vac_rank[:, None])
    receive = jnp.sum(jnp.where(match_table, top_ids[None, :], 0), axis=1)
    return (receive, vacated)


def per_device(matrix, pivots, lower_inverse, upper_inverse):
    shape_in = matrix.shape
    row_blocks = shape_in[0]
    block_size = shape_in[2]
    col_blocks = shape_in[3]
    local_tile = matrix.reshape(row_blocks * block_size, col_blocks * block_size)
    prow_count = lax.axis_size("prow")
    pcol_count = lax.axis_size("pcol")
    prow_index = lax.axis_index("prow")
    pcol_index = lax.axis_index("pcol")
    local_rows = jnp.arange(row_blocks * block_size, dtype=jnp.int32)
    rows_global = (
        local_rows // block_size * prow_count + prow_index
    ) * block_size + local_rows % block_size
    local_cols = jnp.arange(col_blocks * block_size, dtype=jnp.int32)
    cols_global = (
        local_cols // block_size * pcol_count + pcol_index
    ) * block_size + local_cols % block_size
    for step_index in range(PANELS):
        first_row = step_index * block_size
        past_row = first_row + block_size
        sources = pivots[step_index]
        receive, vacated = pairing(sources, first_row, block_size)
        src_block = sources // block_size
        owner_row = src_block % prow_count
        src_local = src_block // prow_count * block_size + sources % block_size
        owned_row = owner_row == prow_index
        picked = jnp.take(local_tile, jnp.where(owned_row, src_local, 0), axis=0)
        contrib = jnp.where(owned_row[:, None], picked, jnp.zeros_like(picked))
        diag_row = step_index % prow_count
        diag_local = step_index // prow_count
        own_top = local_tile[diag_local * block_size : (diag_local + 1) * block_size]
        old_top = from_root(own_top, "prow", diag_row)
        hit_table = (rows_global[:, None] == sources[None, :]) & vacated[None, :]
        hit_rows = jnp.any(hit_table, axis=1)
        giver_row = jnp.sum(jnp.where(hit_table, receive[None, :] - first_row, 0), axis=1)
        local_tile = jnp.where(hit_rows[:, None], jnp.take(old_top, giver_row, axis=0), local_tile)
        cols_right = cols_global >= past_row
        top_rows = lax.psum(contrib, "prow").astype(jnp.float32).astype(jnp.bfloat16)
        upper_rows = jnp.dot(
            lower_inverse[step_index], top_rows, preferred_element_type=jnp.float32
        ).astype(jnp.bfloat16)
        row_block = jnp.where(cols_right[None, :], upper_rows, top_rows)
        update = jnp.where(cols_right[None, :], row_block, jnp.zeros_like(row_block))
        root_col = step_index % pcol_count
        panel_local = step_index // pcol_count
        below_rows = rows_global >= past_row
        panel_raw = local_tile[:, panel_local * block_size : (panel_local + 1) * block_size]
        is_root = pcol_index == root_col

        def compute():
            product = jnp.dot(
                panel_raw, upper_inverse[step_index], preferred_element_type=jnp.float32
            ).astype(jnp.bfloat16)
            return jnp.where(below_rows[:, None], product, jnp.zeros_like(product))

        def nothing():
            return jnp.zeros_like(panel_raw)

        factor = from_root(lax.cond(is_root, compute, nothing), "pcol", root_col)
        local_tile = (
            local_tile.astype(jnp.float32)
            - jnp.dot(factor, update, preferred_element_type=jnp.float32)
        ).astype(jnp.bfloat16)
        updated_slab = local_tile[:, panel_local * block_size : (panel_local + 1) * block_size]
        stored = jnp.where(below_rows[:, None] & is_root, factor, updated_slab)
        local_tile = local_tile.at[
            :, panel_local * block_size : (panel_local + 1) * block_size
        ].set(stored)
        is_diag = prow_index == diag_row
        current = local_tile[diag_local * block_size : (diag_local + 1) * block_size]
        local_tile = local_tile.at[diag_local * block_size : (diag_local + 1) * block_size].set(
            jnp.where(is_diag, row_block, current)
        )
    return local_tile.reshape(shape_in)


def solution(mesh):
    return jax.shard_map(
        per_device,
        mesh=mesh,
        in_specs=(P(None, "prow", None, None, "pcol", None), P(), P(), P()),
        out_specs=P(None, "prow", None, None, "pcol", None),
        check_vma=False,
    )
```

profile of v0, /device:TPU:1, one launch (start us, length us, event | category | flops | bytes accessed | tf_op | source)
XLA Modules:
  0.0 648.5 jit_solution(6534921439675607615)
XLA Ops:
  6.5 0.8 fusion.64
  7.3 2.1 copy.57
  9.5 2.1 gather_fusion
  11.6 1.3 copy.37
  12.9 2.2 broadcast_select_fusion
  15.1 1.3 copy.58
  16.3 1.1 select_select_fusion.5
  17.6 0.2 fusion.21
  17.8 2.6 copy.52
  20.3 0.3 compare_reduce_fusion
  20.6 0.3 reduce-window.48
  20.9 0.1 slice.148
  21.0 0.1 slice_reduce_fusion.1
  21.1 0.3 reduce-window.50
  21.5 0.1 slice.150
  21.6 0.1 slice_reduce_fusion
  21.7 0.3 reduce-window.34
  22.0 0.1 slice.141
  22.1 0.1 slice_reduce_fusion.3
  22.2 0.3 reduce-window.36
  22.5 0.1 slice.143
  22.6 0.1 slice_reduce_fusion.2
  22.8 0.1 add_bitcast_fusion
  22.8 0.1 add_bitcast_fusion.2
  22.9 0.4 select_reduce_fusion.2
  23.3 0.7 fusion.9
  24.0 0.4 select_reduce_fusion.3
  24.4 1.0 select_reduce_fusion
  25.4 117.9 %all-reduce.13.cloned.1.call-done = (bf16[512,1024]{1,0:T(8,128)(2,1)}, bf16[512,1024]{0,1:T(8,128)(2,1)}) async-done(((bf16[512,1024]{1,0:T(8,128)(2,1)}, bf16[512,1024]{0,1:T(8,128)(2,1)}), (bf16[512,1024]{1,0:T(8,128)(2,1)}, bf16[512,1024]{0,1:T(8,128)(2,1)})) %all-reduce.13.cloned.1.call-update) | async-done | bytes 2097168 | tf_op jit(solution)/shard_map/psum | solution.py:11
  143.3 6.3 gather_fusion.1
  149.6 2.6 copy.38
  152.2 2.5 select_select_fusion.1
  154.7 7.0 %conditional.2 = (bf16[1024,512]{0,1:T(8,128)(2,1)S(1)}) conditional(s32[]{:T(128)} %convert_element_type.75, () %tuple.35, (pred[1024]{0:T(1024)(128)(4,1)S(1)}, bf16[2,512,512]{2,1,0:T(8,128)(2,1)}, bf16[1024,1024]{0,1:T(8,128)(2,1)S(1)}) %tuple.36), branch_computations={%region_11.14_spmd, %region_12.15_spmd} | conditional | flops 537919488 | bytes 13108260 | solution.py:85
  154.7 2.6 copy.39
  157.3 2.9 fusion
  160.2 1.5 copy.54
  161.7 1.0 broadcast_select_fusion.2
  162.7 0.2 all-reduce.11.cloned.1.call-start
  163.0 0.7 compare_reduce_fusion.3
  163.7 2.4 fusion.11
  166.1 147.3 %all-reduce.7.cloned.1.call-done = bf16[1024,512]{0,1:T(8,128)(2,1)} async-done(((bf16[1024,512]{0,1:T(8,128)(2,1)}), bf16[1024,512]{0,1:T(8,128)(2,1)}) %all-reduce.7.cloned.1.call-update) | async-done | bytes 1048592 | tf_op jit(solution)/shard_map/psum | solution.py:11
  313.4 2.6 subtract_convert_fusion.1
  316.0 1.1 fusion.14
  317.2 1.7 broadcast_select_fusion.3
  318.9 1.3 copy-done
  320.2 2.9 copy.46
  323.1 2.1 gather_fusion.3
  325.2 0.5 copy.47
  325.7 1.1 select_select_fusion.4
  326.9 121.9 %all-reduce.11.cloned.1.call-done = (bf16[512,1024]{0,1:T(8,128)(2,1)}, bf16[512,1024]{0,1:T(8,128)(2,1)}) async-done(((bf16[512,1024]{0,1:T(8,128)(2,1)}, bf16[512,1024]{0,1:T(8,128)(2,1)}), (bf16[512,1024]{0,1:T(8,128)(2,1)}, bf16[512,1024]{0,1:T(8,128)(2,1)})) %all-reduce.11.cloned.1.call-update) | async-done | bytes 2097168 | tf_op jit(solution)/shard_map/psum | solution.py:11
  448.8 1.5 copy.42
  450.3 5.4 gather_fusion.2
  455.7 4.1 copy.43
  459.8 3.1 select_select_fusion
  462.9 0.1 conditional.3
  462.9 0.1 broadcast.557.clone
  463.1 1.1 broadcast_select_fusion.1
  464.2 2.6 fusion.13
  466.8 154.8 %all-reduce.9.cloned.1.call-done = bf16[1024,512]{0,1:T(8,128)(2,1)} async-done(((bf16[1024,512]{0,1:T(8,128)(2,1)}), bf16[1024,512]{0,1:T(8,128)(2,1)}) %all-reduce.9.cloned.1.call-update) | async-done | bytes 1048592 | tf_op jit(solution)/shard_map/psum | solution.py:11
  621.7 3.9 subtract_convert_fusion
  625.6 3.3 fusion.15
  628.9 2.5 fusion.16
  631.3 3.3 reshape.401
  634.7 7.3 %copy.49 = bf16[2,1,512,2,1,512]{5,3,4,2,1,0:T(2,128)(2,1)} copy(bf16[2,1,512,2,1,512]{2,0,5,3,4,1:T(2,128)(2,1)S(1)} %reshape.401) | data formatting | bytes 4194304 | tf_op jit(solution)/shard_map/reshape | solution.py:100
  (44 shorter events, 0.5 us)
Async XLA Ops:
  6.5 136.7 %all-reduce.13.cloned.1.call-start = ((), (), s32[]{:S(2)}) async-start(), calls=%async_computation.3 | async-start | bytes 4194304 | tf_op jit(solution)/shard_map/psum | solution.py:11
  12.9 3.4 copy-start.3
  16.3 1.2 copy-start.6
  17.5 295.9 %all-reduce.7.cloned.1.call-start = ((), (), s32[]{:S(2)}) async-start(), calls=%async_computation | async-start | bytes 2097152 | tf_op jit(solution)/shard_map/psum | solution.py:11
  154.7 2.6 copy-start.7
  162.7 286.1 %all-reduce.11.cloned.1.call-start = ((), (), s32[]{:S(2)}) async-start(), calls=%async_computation.2 | async-start | bytes 4194304 | tf_op jit(solution)/shard_map/psum | solution.py:11
  313.4 2.6 copy-start.4
  318.9 1.3 copy-start
  326.8 294.8 %all-reduce.9.cloned.1.call-start = ((), (), s32[]{:S(2)}) async-start(), calls=%async_computation.1 | async-start | bytes 2097152 | tf_op jit(solution)/shard_map/psum | solution.py:11
  455.7 4.1 copy-start.1
  464.2 157.5 %copy-start.2 = (bf16[1024,1024]{0,1:T(8,128)(2,1)S(1)}, bf16[1024,1024]{0,1:T(8,128)(2,1)}, u32[]{:S(2)}) copy-start(bf16[1024,1024]{0,1:T(8,128)(2,1)} %select_select_fusion) | copy-start | bytes 6291460
  621.7 3.9 copy-start.5
Sparse Core Ops, SparseCore 0:
  17.6 125.6 all-reduce.12
  162.9 150.4 all-reduce.6
  327.0 121.8 all-reduce.10
  464.3 157.3 all-reduce.8
where the time goes:
time: 653 us; the launch traced here: 648 us
  waiting for transfers between devices  542 us (83%)
  local copies, waits for them, and re-layouts  52.3 us (8%)
  other arithmetic  26 us (4%)
  matrix products  14.5 us (2%)
  between operations  13.4 us (2%)
    psum x4, waiting for transfers between devices, from_root(): return lax.psum(jnp.where(mine, value, jnp.zeros_like(value)), axis)  542 us
    gather x4, local copies, waits for them, and re-layouts, per_device(): jnp.take(old_top, giver_row, axis=0)  18.4 us
  transfers between devices with their start and end apart: 4, of which 4 were waited for; matrix products, arithmetic and copies ran while one was open for 2% of the time, Pallas kernels for 0%

commit v1 on v0

v1 whole, which is shorter than its diff:
```python
import jax
import jax.numpy as jnp
from jax import lax
from jax.experimental import pallas as pl
from jax.experimental.pallas import tpu as pltpu
from jax.sharding import PartitionSpec as P

NB = 512
CORES = 2
NX = 4
CAP = 96
DCAP = 56
PA = 16
PB = 24
MESH = pl.DeviceIdType.MESH
ANY = pl.BlockSpec(memory_space=pl.ANY)


class Ring:
    def __init__(self, n, pos, goto, item, send, recv, fresh=None, arrived=None):
        self.n, self.pos, self.goto, self.item = n, pos, goto, item
        self.send, self.recv = send, recv
        self.fresh, self.arrived = fresh, arrived
        self.got = [0, 0]

    def carries(self, way, hop, half):
        return hop < self.n // 2 or (hop == self.n // 2 and half == way)

    def copy(self, way, hop, half):
        step = 1 if way == 0 else -1
        index = lax.rem(self.pos + self.n - step * (hop - 1), self.n)
        target = lax.rem(self.pos + self.n + step, self.n)
        src = self.item(index, half)
        if hop == 1 and self.fresh is not None:
            src = self.fresh(half)
        return pltpu.make_async_remote_copy(
            src_ref=src,
            dst_ref=self.item(index, half),
            send_sem=self.send.at[way, hop - 1, half],
            recv_sem=self.recv.at[way, hop - 1, half],
            device_id=self.goto(target),
            device_id_type=MESH,
        )

    def landed(self, way, hop, half):
        step = 1 if way == 0 else -1
        index = lax.rem(self.pos + self.n - step * hop, self.n)
        ref = self.item(index, half)
        return index, ref, pltpu.make_async_remote_copy(
            src_ref=ref,
            dst_ref=ref,
            send_sem=self.send.at[way, hop - 1, half],
            recv_sem=self.recv.at[way, hop - 1, half],
            device_id=self.goto(lax.rem(self.pos + 1, self.n)),
            device_id_type=MESH,
        )

    def start(self, half):
        for way in (0, 1):
            self.copy(way, 1, half).start()

    def step(self, way, hop, half):
        index, ref, arrival = self.landed(way, hop, half)
        arrival.wait_recv()
        if self.carries(way, hop + 1, half):
            self.copy(way, hop + 1, half).start()
        self.got[half] += 1
        if self.arrived is not None:
            self.arrived(index, ref, way, hop, half)

    def events(self, t0, dt):
        out = []
        for half in (0, 1):
            for hop in range(1, self.n // 2 + 1):
                for way in (0, 1):
                    if self.carries(way, hop, half):
                        when = t0[half] + dt * hop
                        out.append((when, lambda w=way, h=hop, f=half: self.step(w, h, f)))
        return out

    def complete(self, half):
        assert self.got[half] == self.n - 1

    def drain(self):
        for half in (0, 1):
            for hop in range(1, self.n // 2 + 1):
                for way in (0, 1):
                    if self.carries(way, hop, half):
                        self.copy(way, hop, half).wait_send()


def run_events(events):
    for _, act in sorted(events, key=lambda e: e[0]):
        act()


class RowExchange:
    def __init__(self, ny, sent, spread, rows, moved, sems):
        self.ny, self.sent, self.spread, self.rows, self.moved = ny, sent, spread, rows, moved
        (self.rs, self.rr, self.fs, self.fr, self.os, self.orr, self.ls, self.es, self.er) = sems
        prow = lax.axis_index("prow")
        self.y, self.c = lax.div(prow, CORES), lax.rem(prow, CORES)
        self.partner = {"prow": self.y * CORES + 1 - self.c}
        self.ring = Ring(
            ny, self.y,
            lambda i: {"prow": i * CORES + self.c},
            lambda i, half: rows.at[i * CORES + self.c, half],
            self.rs, self.rr,
            fresh=lambda half: sent.at[half],
            arrived=self.forward,
        )
        self.forwards = []

    def barrier_peers(self):
        ids = [{"prow": lax.rem(self.y + k, self.ny) * CORES + c} for k in range(1, self.ny) for c in (0, 1)]
        return ids + [self.partner]

    def forward_copy(self, index, way, hop, half):
        return pltpu.make_async_remote_copy(
            src_ref=self.rows.at[index * CORES + self.c, half],
            dst_ref=self.rows.at[index * CORES + self.c, half],
            send_sem=self.fs.at[way, hop - 1, half],
            recv_sem=self.fr.at[way, hop - 1, half],
            device_id=self.partner,
            device_id_type=MESH,
        )

    def forward(self, index, ref, way, hop, half):
        copy = self.forward_copy(index, way, hop, half)
        copy.start()
        self.forwards.append((copy, index, way, hop, half))

    def own_copies(self):
        mine = self.rows.at[self.y * CORES + self.c]
        local = pltpu.make_async_copy(self.sent, mine, self.ls.at[0])
        across = pltpu.make_async_remote_copy(
            src_ref=self.sent, dst_ref=mine, send_sem=self.os, recv_sem=self.orr,
            device_id=self.partner, device_id_type=MESH,
        )
        return local, across

    def spread_copy(self, k, core):
        to = lax.rem(self.y + k, self.ny) * CORES + core
        return pltpu.make_async_remote_copy(
            src_ref=self.spread.at[to], dst_ref=self.moved.at[self.c],
            send_sem=self.es.at[k, core], recv_sem=self.er.at[self.c],
            device_id={"prow": to}, device_id_type=MESH,
        )

    def spread_partner(self):
        to = 1 - self.c
        return pltpu.make_async_remote_copy(
            src_ref=self.spread.at[to], dst_ref=self.moved.at[self.c],
            send_sem=self.es.at[0, 0], recv_sem=self.er.at[self.c],
            device_id=self.partner, device_id_type=MESH,
        )

    def spread_own(self):
        return pltpu.make_async_copy(self.spread.at[self.c], self.moved.at[self.c], self.er.at[self.c])

    def begin(self):
        for half in (0, 1):
            self.ring.start(half)
        for copy in self.own_copies():
            copy.start()

    def spread_some(self, ks):
        @pl.when(self.y == 0)
        def _():
            for k in ks:
                for core in (0, 1):
                    self.spread_copy(k, core).start()

    def spread_near(self):
        @pl.when(self.y == 0)
        def _():
            self.spread_partner().start()
            self.spread_own().start()

    def events(self, dt):
        half_n = self.ny // 2
        out = [(-1.0, self.begin), (3.9 * dt, self.spread_near)]
        order = [half_n] + [k for d in range(half_n - 1, 0, -1) for k in (d, self.ny - d)]
        for i, k in enumerate(order):
            out.append((0.1 + i * 0.5 * dt, lambda k=k: self.spread_some([k])))
        return out + self.ring.events([0.0, 0.3 * dt], dt)

    def finish(self):
        local, across = self.own_copies()
        local.wait()
        across.wait()
        self.ring.drain()
        for copy, index, way, hop, half in self.forwards:
            copy.wait_send()
        for copy, index, way, hop, half in self.forwards:
            ref = self.rows.at[index * CORES + 1 - self.c, half]
            pltpu.make_async_remote_copy(
                src_ref=ref, dst_ref=ref,
                send_sem=self.fs.at[way, hop - 1, half], recv_sem=self.fr.at[way, hop - 1, half],
                device_id=self.partner, device_id_type=MESH,
            ).wait_recv()
        for core in (0, 1):
            ref = self.moved.at[core]
            pltpu.make_async_copy(ref, ref, self.er.at[core]).wait()

        @pl.when(self.y == 0)
        def _():
            for k in range(1, self.ny):
                for core in (0, 1):
                    self.spread_copy(k, core).wait_send()
            self.spread_partner().wait_send()


def exchange_sems(ny):
    dma = pltpu.SemaphoreType.DMA
    return [
        dma((2, ny // 2, 2)), dma((2, ny // 2, 2)),
        dma((2, ny // 2, 2)), dma((2, ny // 2, 2)),
        dma, dma, dma((1,)), dma((ny, CORES)), dma((CORES,)),
    ]


def meet(peers):
    barrier = pltpu.get_barrier_semaphore()
    for peer in peers:
        pl.semaphore_signal(barrier, inc=1, device_id=peer, device_id_type=MESH)
    pl.semaphore_wait(barrier, len(peers))


def exchange_kernel(ny, sent, spread, rows, moved, *sems):
    ex = RowExchange(ny, sent, spread, rows, moved, sems)
    meet(ex.barrier_peers())
    run_events(ex.events(3.8))
    ex.finish()


def row_exchange(sent, spread, ny, cid):
    width = sent.shape[-1]
    return pl.pallas_call(
        lambda *refs: exchange_kernel(ny, *refs),
        out_shape=(
            jax.ShapeDtypeStruct((ny * CORES, 2, CAP // 2, width), jnp.bfloat16),
            jax.ShapeDtypeStruct((CORES, DCAP, width), jnp.bfloat16),
        ),
        in_specs=[ANY, ANY],
        out_specs=(ANY, ANY),
        scratch_shapes=exchange_sems(ny),
        compiler_params=pltpu.CompilerParams(collective_id=cid, has_side_effects=True),
        name="row_exchange_%d" % cid,
    )(sent, spread)


def spread_kernel(ny, nz, nexch, *refs):
    src_a, src_b, sent, spread, buf_a, buf_b, other, rows, moved = refs[:9]
    sems = refs[9 : 9 + nexch]
    (axs, axr, azs, azr, bzs, bzr, bxs, bxr, ss, sr, ts, tr) = refs[9 + nexch :]
    ex = RowExchange(ny, sent, spread, rows, moved, sems)
    pcol = lax.axis_index("pcol")
    n = nz * NX
    z, x = lax.div(pcol, NX), lax.rem(pcol, NX)

    barrier = pltpu.get_barrier_semaphore()

    def signal(peer):
        pl.semaphore_signal(barrier, inc=1, device_id=peer, device_id_type=MESH)

    near = ex.barrier_peers()
    near += [{"pcol": z * NX + lax.rem(x + d, NX)} for d in (1, NX - 1)]
    near += [{"pcol": lax.rem(z + d, nz) * NX + x} for d in (1, nz - 1)]
    for peer in near:
        signal(peer)
    for root in (0, 1):
        @pl.when(pcol == root)
        def _():
            for k in range(1, n):
                signal({"pcol": lax.rem(pcol + k, n)})

        @pl.when(pcol != root)
        def _():
            signal({"pcol": root})

    @pl.when(pcol < 2)
    def _():
        pl.semaphore_wait(barrier, len(near) + n)

    @pl.when(pcol >= 2)
    def _():
        pl.semaphore_wait(barrier, len(near) + 2)

    def scatter_copies(k):
        to = lax.rem(pcol + k, n)
        tz, tx = lax.div(to, NX), lax.rem(to, NX)
        args = dict(device_id={"pcol": to}, device_id_type=MESH)
        a = pltpu.make_async_remote_copy(
            src_ref=src_a.at[tz, tx], dst_ref=buf_a.at[pcol, tz, tx],
            send_sem=ss.at[k, 0], recv_sem=sr.at[0, pcol], **args)
        b = pltpu.make_async_remote_copy(
            src_ref=src_b.at[tx, tz], dst_ref=buf_b.at[pcol, tx, tz],
            send_sem=ss.at[k, 1], recv_sem=sr.at[1, pcol], **args)
        return a, b

    def scatter():
        @pl.when(pcol < 2)
        def _():
            for which in (0, 1):
                for k in range(1, n):
                    scatter_copies(k)[which].start()
            pltpu.make_async_copy(src_a.at[z, x], buf_a.at[pcol, z, x], sr.at[0, pcol]).start()
            pltpu.make_async_copy(src_b.at[x, z], buf_b.at[pcol, x, z], sr.at[1, pcol]).start()

    def to_x(i):
        return {"pcol": z * NX + i}

    def to_z(i):
        return {"pcol": i * NX + x}

    ax = Ring(NX, x, to_x, lambda i, h: buf_a.at[h, z, i], axs, axr)
    az = Ring(nz, z, to_z, lambda i, h: buf_a.at[h, i], azs, azr)
    bz = Ring(nz, z, to_z, lambda i, h: buf_b.at[h, x, i], bzs, bzr)
    bx = Ring(NX, x, to_x, lambda i, h: buf_b.at[h, i], bxs, bxr)

    def own(which, half):
        ref = buf_a.at[half, z, x] if which == 0 else buf_b.at[half, x, z]
        pltpu.make_async_copy(ref, ref, sr.at[which, half]).wait()

    def begin(ring, half, which=None, after=None):
        if which is not None:
            own(which, half)
        if after is not None:
            after.complete(half)
        ring.start(half)

    def across(half):
        return pltpu.make_async_remote_copy(
            src_ref=buf_a.at[half, pl.ds(0, nz // 2)], dst_ref=other.at[half],
            send_sem=ts.at[half], recv_sem=tr.at[half],
            device_id=ex.partner, device_id_type=MESH)

    def send_other(half):
        az.complete(half)
        across(half).start()

    events = [(-0.5, scatter)]
    events += ex.events(3.8)
    events += [(5.0 + h * 0.1, lambda h=h: begin(ax, h, which=0)) for h in (0, 1)]
    events += ax.events([5.0, 5.2], 1.8)
    events += [(7.0 + h * 0.1, lambda h=h: begin(bz, h, which=1)) for h in (0, 1)]
    events += bz.events([7.2, 7.4], 2.2)
    events += [(9.0 + h * 0.1, lambda h=h: begin(az, h, after=ax)) for h in (0, 1)]
    events += az.events([9.2, 9.5], 3.4)
    events += [(16.5 + h * 0.1, lambda h=h: begin(bx, h, after=bz)) for h in (0, 1)]
    events += bx.events([17.0, 18.0], 6.0)
    events += [(25.0 + h * 0.1, lambda h=h: send_other(h)) for h in (0, 1)]
    run_events(events)
    ex.finish()
    for ring in (ax, az, bz, bx):
        for half in (0, 1):
            ring.complete(half)
        ring.drain()
    for half in (0, 1):
        across(half).wait()

    @pl.when(pcol < 2)
    def _():
        for k in range(1, n):
            for copy in scatter_copies(k):
                copy.wait_send()


def panel_spread(src_a, src_b, sent, spread, ny, nz, cid):
    width = sent.shape[-1]
    dma = pltpu.SemaphoreType.DMA
    sems = exchange_sems(ny)
    return pl.pallas_call(
        lambda *refs: spread_kernel(ny, nz, len(sems), *refs),
        out_shape=(
            jax.ShapeDtypeStruct((2, nz, NX, PA, NB), jnp.bfloat16),
            jax.ShapeDtypeStruct((2, NX, nz, PB, NB), jnp.bfloat16),
            jax.ShapeDtypeStruct((2, nz // 2, NX, PA, NB), jnp.bfloat16),
            jax.ShapeDtypeStruct((ny * CORES, 2, CAP // 2, width), jnp.bfloat16),
            jax.ShapeDtypeStruct((CORES, DCAP, width), jnp.bfloat16),
        ),
        in_specs=[ANY] * 4,
        out_specs=(ANY,) * 5,
        scratch_shapes=sems
        + [dma((2, NX // 2, 2)), dma((2, NX // 2, 2)), dma((2, nz // 2, 2)), dma((2, nz // 2, 2))]
        + [dma((2, nz // 2, 2)), dma((2, nz // 2, 2)), dma((2, NX // 2, 2)), dma((2, NX // 2, 2))]
        + [dma((nz * NX, 2)), dma((2, 2)), dma((2,)), dma((2,))],
        compiler_params=pltpu.CompilerParams(collective_id=cid, has_side_effects=True),
        name="panel_spread_%d" % cid,
    )(src_a, src_b, sent, spread)


def count_before(flags):
    n = flags.shape[0]
    ahead = jnp.arange(n)[None, :] < jnp.arange(n)[:, None]
    return jnp.sum((ahead & flags[None, :]).astype(jnp.int32), axis=1)


def pairing(sources, first_row):
    top_ids = first_row + jnp.arange(NB, dtype=jnp.int32)
    leftover = jnp.logical_not(jnp.any(sources[None, :] == top_ids[:, None], axis=1))
    left_rank = count_before(leftover)
    vacated = sources >= first_row + NB
    vac_rank = count_before(vacated)
    table = leftover[None, :] & (left_rank[None, :] == vac_rank[:, None])
    return jnp.sum(jnp.where(table, top_ids[None, :], 0), axis=1)


def lookup(keys, names, values):
    hit = keys[:, None] == names[None, :]
    found = jnp.sum(jnp.where(hit, values[None, :], 0), axis=1)
    return jnp.where(jnp.any(hit, axis=1), found, keys)


def rank_in(group):
    n = group.shape[0]
    ahead = jnp.arange(n)[None, :] < jnp.arange(n)[:, None]
    same = group[None, :] == group[:, None]
    return jnp.sum((same & ahead).astype(jnp.int32), axis=1)


def slot_values(keys, values, wanted):
    hit = wanted[:, None] == keys[None, :]
    return jnp.sum(jnp.where(hit, values[None, :] + 1, 0), axis=1) - 1


def one_hot(index, n):
    return (index[:, None] == jnp.arange(n, dtype=jnp.int32)[None, :]).astype(jnp.bfloat16)


def dot(a, b):
    return jnp.dot(a, b, preferred_element_type=jnp.float32)


def bdot(a, b):
    return dot(a, b).astype(jnp.bfloat16)


def per_device(matrix, pivots, lower_inverse, upper_inverse):
    nprow, npcol = lax.axis_size("prow"), lax.axis_size("pcol")
    ny, nz = nprow // CORES, npcol // NX
    prow, pcol = lax.axis_index("prow"), lax.axis_index("pcol")
    core = lax.rem(prow, CORES)
    tiles = [matrix[:, 0, :, d, 0, :].reshape(2 * NB, NB) for d in (0, 1)]

    s0, s1 = pivots[0], pivots[1]
    receive0, receive1 = pairing(s0, 0), pairing(s1, NB)
    src1 = lookup(s1, s0, receive0)
    from1 = lookup(receive1, s0, receive0)
    again = jnp.any(s0[:, None] == s1[None, :], axis=1)
    big = jnp.int32(1 << 20)

    def owner(rows):
        return lax.rem(rows // NB, nprow)

    def local(rows):
        return rows // (NB * nprow) * NB + lax.rem(rows, NB)

    t_src = jnp.concatenate([s0, src1])
    t_owner = owner(t_src)
    t_rank = rank_in(t_owner)
    t_local = local(t_src)
    d_dst = jnp.concatenate([s0, s1])
    d_src = jnp.concatenate([receive0, from1])
    d_valid = (d_dst >= 2 * NB) & jnp.concatenate([jnp.logical_not(again), jnp.ones((NB,), jnp.bool_)])
    d_core = d_src // NB
    d_owner = owner(d_dst)
    d_rank = rank_in(jnp.where(d_valid, d_owner * CORES + d_core, -1))
    d_local = local(d_dst)
    rounds = jnp.maximum(
        jnp.max(t_rank) // CAP, jnp.max(jnp.where(d_valid, d_rank, 0)) // DCAP
    ) + 1

    def plan(r):
        t_in = (t_rank // CAP) == r
        t_slot = t_owner * CAP + lax.rem(t_rank, CAP)
        d_in = d_valid & ((d_rank // DCAP) == r)
        d_slot = (d_owner * CORES + d_core) * DCAP + lax.rem(d_rank, DCAP)
        t_key = jnp.where(t_in, t_slot, big)
        d_key = jnp.where(d_in, d_slot, big)
        send_sel = one_hot(slot_values(t_key, t_local, prow * CAP + jnp.arange(CAP, dtype=jnp.int32)), 2 * NB)
        place = one_hot(jnp.where(t_in, t_slot, -1), nprow * CAP)
        every = jnp.arange(nprow * DCAP, dtype=jnp.int32)
        wanted = (every // DCAP * CORES + core) * DCAP + lax.rem(every, DCAP)
        spread_sel = one_hot(lax.rem(slot_values(d_key, d_src + NB, wanted), NB + 0) * 1, NB)
        have = slot_values(d_key, d_src, wanted) >= 0
        spread_sel = jnp.where(have[:, None], spread_sel, jnp.zeros_like(spread_sel))
        mine = prow * CORES * DCAP + jnp.arange(CORES * DCAP, dtype=jnp.int32)
        into = slot_values(d_key, d_local, mine)
        insert = (jnp.arange(2 * NB, dtype=jnp.int32)[:, None] == into[None, :]).astype(jnp.bfloat16)
        hit = jnp.any(insert > 0, axis=1)
        return send_sel, place, spread_sel, insert, hit

    def pack(sel, spread_sel, tile):
        width = tile.shape[1]
        sent = bdot(sel, tile).reshape(2, CAP // 2, width)
        spread = lax.cond(
            prow < CORES,
            lambda: bdot(spread_sel, tile[:NB]),
            lambda: jnp.zeros((nprow * DCAP, width), jnp.bfloat16),
        ).reshape(nprow, DCAP, width)
        return sent, spread

    def unpack_rows(place, rows):
        return bdot(place, rows.reshape(nprow * CAP, rows.shape[-1]))

    def unpack_moved(insert, hit, moved, tile):
        new = bdot(insert, moved.reshape(CORES * DCAP, moved.shape[-1]))
        return jnp.where(hit[:, None], new, tile)

    send_sel, place, spread_sel, insert, hit = plan(0)
    packs = [pack(send_sel, spread_sel, tile) for tile in tiles]
    rows0, moved0 = row_exchange(*packs[0], ny, 0)
    top0 = unpack_rows(place, rows0)
    tile0 = unpack_moved(insert, hit, moved0, tiles[0])

    def more(top0, tile0):
        whole = jnp.concatenate(tiles, axis=1)

        def body(state):
            r, top, tile = state
            send_sel, place, spread_sel, insert, hit = plan(r)
            rows, moved = row_exchange(*pack(send_sel, spread_sel, whole), ny, 1)
            return r + 1, top + unpack_rows(place, rows), unpack_moved(insert, hit, moved, tile)

        start = jnp.concatenate([top0, jnp.zeros_like(top0)], axis=1), jnp.concatenate([tile0, tiles[1]], axis=1)
        _, top, tile = lax.while_loop(lambda s: s[0] < rounds, body, (jnp.int32(1),) + start)
        return top[:, :NB], top[:, NB:], tile[:, :NB], tile[:, NB:]

    def none(top0, tile0):
        return top0, jnp.zeros_like(top0), tile0, tiles[1]

    top0, extra, tile0, tile1 = lax.cond(rounds > 1, more, none, top0, tile0)

    panel_top = jnp.where(pcol == 0, top0[NB:], top0[:NB])
    quarter = NB // CORES
    part = lax.dynamic_slice_in_dim(panel_top, core * quarter, quarter, 0)
    src_a = jnp.concatenate([part, tile0[:quarter]], axis=0).reshape(nz, NX, PA, NB)
    src_b = tile0[quarter:].reshape(NX, nz, PB, NB)
    buf_a, buf_b, other, rows1, moved1 = panel_spread(src_a, src_b, *packs[1], ny, nz, 2)

    top1 = unpack_rows(place, rows1) + extra
    tile1 = unpack_moved(insert, hit, moved1, tile1)
    flat_a = buf_a.reshape(2, NB, NB)
    flat_b = buf_b.reshape(2, 2 * NB - quarter, NB)
    other = other.reshape(2, quarter, NB)
    raw = [jnp.concatenate([flat_a[k, quarter:], flat_b[k]], axis=0) for k in (0, 1)]
    first = jnp.where(core == 0, flat_a[:, :quarter], other)
    second = jnp.where(core == 0, other, flat_a[:, :quarter])
    tops = jnp.concatenate([first, second], axis=1)

    l0, l1, u0, u1 = lower_inverse[0], lower_inverse[1], upper_inverse[0], upper_inverse[1]
    factor0 = bdot(raw[0], u0)
    corner = bdot(tops[0], u0)
    upper_panel = bdot(l0, tops[1])
    panel1 = (raw[1].astype(jnp.float32) - dot(factor0, upper_panel)).astype(jnp.bfloat16)
    factor1 = bdot(panel1, u1)
    out = []
    for d, (top, tile) in enumerate(((top0, tile0), (top1, tile1))):
        up0 = bdot(l0, top[:NB])
        low = (top[NB:].astype(jnp.float32) - dot(corner, up0)).astype(jnp.bfloat16)
        up1 = bdot(l1, low)
        new = (tile.astype(jnp.float32) - dot(factor0, up0)).astype(jnp.bfloat16)
        new = (new.astype(jnp.float32) - dot(factor1, up1)).astype(jnp.bfloat16)
        row0, row1 = up0, up1
        if d == 0:
            new = jnp.where(pcol == 0, factor0, jnp.where(pcol == 1, factor1, new))
            row0 = jnp.where(pcol == 0, top[:NB], up0)
            row1 = jnp.where(pcol == 0, corner, jnp.where(pcol == 1, low, up1))
        head = jnp.where(prow == 0, row0, jnp.where(prow == 1, row1, new[:NB]))
        out.append(jnp.concatenate([head, new[NB:]], axis=0).reshape(2, NB, NB))
    return jnp.stack(out, axis=2).reshape(matrix.shape)


def solution(mesh):
    return jax.shard_map(
        per_device,
        mesh=mesh,
        in_specs=(P(None, "prow", None, None, "pcol", None), P(), P(), P()),
        out_specs=P(None, "prow", None, None, "pcol", None),
        check_vma=False,
    )
```

time: 653 us -> 174 us (0.27)
  waiting for transfers between devices: 542 us -> 0 us
  Pallas kernels: 0 us -> 90.4 us
  local copies, waits for them, and re-layouts: 52.3 us -> 24.2 us
  matrix products: 14.5 us -> 35.2 us
  between operations: 13.4 us -> 4.53 us
  other arithmetic: 26 us -> 17.7 us
    psum x4 -> x0, waiting for transfers between devices: 542 us -> none  [from_root(): return lax.psum(jnp.where(mine, value, jnp.zeros_like(value)), axis)]
    pallas_call x0 -> x2, Pallas kernels: none -> 90.4 us  [the longest x1 59.7 us: panel_spread(): pl.pallas_call(lambda *refs: spread_kernel(ny, nz, len(sems), *refs), out...]
    gather x8 -> x0, local copies, waits for them, and re-layouts: 24.4 us -> none  [the longest x4 18.4 us: per_device(): jnp.take(old_top, giver_row, axis=0)]
    dot_general x5 -> x21, matrix products: 14.5 us -> 35.2 us  [dot(): return jnp.dot(a, b, preferred_element_type=jnp.float32)]
    reshape x3 -> x0, local copies, waits for them, and re-layouts: 13.1 us -> none  [the longest x2 10.6 us: per_device(): return local_tile.reshape(shape_in)]
    slice x1 -> x6, local copies, waits for them, and re-layouts: 0.77 us -> 10.8 us  [the longest x1 6.53 us: per_device(): tiles = [matrix[:, 0, :, d, 0, :].reshape(2 * NB, NB) for d in (0, 1)]]
    select_n x8 -> x11, other arithmetic: 13.8 us -> 5.09 us  [the longest x2 1.42 us: per_device(): head = jnp.where(prow == 0, row0, jnp.where(prow == 1, row1, new[:NB]))]
    scatter x3 -> x0, other arithmetic: 6.88 us -> none  [the longest x2 4.4 us: per_device(): local_tile = local_tile.at[:, panel_local * block_size:(panel_local + 1)...]
  transfers between devices with their start and end apart: 4 -> 0, of which waited for: 4 -> 0; matrix products, arithmetic and copies ran while one was open for 2% -> 0% of each run, Pallas kernels for 0% -> 0%
where the time goes in v1:
time: 174 us; the launch traced here: 172 us
  Pallas kernels  90.4 us (52%)
  matrix products  35.2 us (20%)
  local copies, waits for them, and re-layouts  24.2 us (14%)
  other arithmetic  17.7 us (10%)
  between operations  4.53 us (3%)
    pallas_call x1, Pallas kernels, panel_spread(): pl.pallas_call(lambda *refs: spread_kernel(ny, nz, len(sems), *refs), out...  59.7 us
    dot_general x21, matrix products, dot(): return jnp.dot(a, b, preferred_element_type=jnp.float32)  35.2 us
    pallas_call x1, Pallas kernels, row_exchange(): pl.pallas_call(lambda *refs: exchange_kernel(ny, *refs), out_shape=(jax.S...  30.7 us
    slice x1, local copies, waits for them, and re-layouts, per_device(): tiles = [matrix[:, 0, :, d, 0, :].reshape(2 * NB, NB) for d in (0, 1)]  6.53 us
    unnamed x52, local copies, waits for them, and re-layouts  6.43 us
    reshape x1, other arithmetic, per_device(): return jnp.stack(out, axis=2).reshape(matrix.shape)  5.63 us
    another operation x2, local copies, waits for them, and re-layouts, per_device(): return jnp.stack(out, axis=2).reshape(matrix.shape)  3.5 us

profile of v1, /device:TPU:1, one launch (start us, length us, event | category | flops | bytes accessed | tf_op | source)
XLA Modules:
  0.0 172.0 jit_solution(17782311565524477509)
XLA Ops:
  0.0 0.8 fusion.140
  0.8 0.3 compare_reduce_fusion.6
  1.0 0.2 convert_reduce_fusion.3
  1.2 0.8 compare_reduce_fusion.9
  2.0 0.2 convert_reduce_fusion.2
  2.2 0.4 select_reduce_fusion.4
  2.6 0.7 compare_reduce_fusion.4
  3.5 0.4 select_reduce_fusion.5
  3.9 0.4 fusion.53
  4.3 0.7 reshape_select_fusion
  5.0 0.5 convert_reduce_fusion
  5.6 0.7 add_select_fusion.16
  6.2 0.8 fusion.38
  7.1 0.3 fusion.63
  7.4 6.5 %fusion.137 = (bf16[2,1,512,1,1,512]{5,3,4,2,1,0:T(2,128)(2,1)}, bf16[2,1,512,1,1,512]{5,3,4,2,1,0:T(2,128)(2,1)S(1)}) fusion(bf16[2,1,512,2,1,512]{5,3,4,2,1,0:T(2,128)(2,1)} %param.14), kind=kLoop, calls=%fused_computation.307 | loop fusion | bytes 4194304 | tf_op jit(solution)/shard_map/slice | solution.py:445
  14.0 0.3 copy.15
  14.3 0.7 conditional.4
  14.3 0.6 convolution_convert_fusion
  14.9 0.5 convert_reduce_fusion.1
  15.5 0.7 add_select_fusion.18
  16.2 0.2 select_reduce_fusion.7
  16.4 1.0 convolution_convert_fusion.15
  17.4 30.7 %row_exchange_0.1 = (bf16[16,2,48,512]{3,2,1,0:T(8,128)(2,1)}, bf16[2,56,512]{2,1,0:T(8,128)(2,1)}) custom-call(bf16[2,48,512]{2,1,0:T(8,128)(2,1)} %bitcast.139, bf16[16,56,512]{2,1,0:T(8,128)(2,1)S(1)} %get-tuple-element.925.refs_1_), custom_call_target="tpu_custom_call" | custom-call | tf_op jit(solution)/shard_map/row_exchange_0/pallas_call | solution.py:239
  48.2 0.2 select_reduce_fusion.6
  48.5 1.6 fusion.46
  50.1 1.8 %fusion.44 = bf16[1024,512]{1,0:T(8,128)(2,1)S(1)} fusion(bf16[1536,512]{1,0:T(8,128)(2,1)S(1)} %bitcast.161, s32[1024]{0:T(1024)S(1)} %get-tuple-element.676), kind=kOutput, calls=%fused_computation.106 | convolution fusion | flops 1612709888 | bytes 2625536 | tf_op jit(solution)/shard_map/dot_general | solution.py:433
  55.9 2.9 %copy.16 = bf16[2,1,512,1,1,512]{5,2,0,4,3,1:T(8,128)(2,1)} copy(bf16[2,1,512,1,1,512]{5,3,4,2,1,0:T(2,128)(2,1)} %get-tuple-element.662) | data formatting | bytes 2097152
  58.9 3.4 %conditional.5 = (bf16[1024,512]{1,0:T(8,128)(2,1)S(1)}, bf16[1024,512]{1,0:T(8,128)(2,1)}, bf16[1024,512]{1,0:T(8,128)(2,1)S(1)}, bf16[1024,512]{1,0:T(8,128)(2,1)}) conditional(s32[]{:T(128)} %convert_element_type.189, (bf16[1024,512]{1,0:T(8,128)(2,1)S(1)}, bf16[1024,512]{1,0:T(8,128)(2,1)S(1)}, bf16[1024,512]{1,0:T(8,128)(2,1)}) %tuple.57, ...), branch_computations={%region_24.25_spmd, %region_25.35_spmd} | conditional | flops 4619577344 | bytes 80618824 | solution.py:534
  58.9 2.3 %copy.33 = bf16[1024,512]{1,0:T(8,128)(2,1)} copy(bf16[1024,512]{1,0:T(8,128)(2,1)} %get-tuple-element.920) | data formatting | bytes 2097152 | tf_op jit(solution)/shard_map/cond
  61.1 1.1 broadcast.827
  62.4 0.8 pad_maximum_fusion.5
  63.3 0.9 slice.114
  64.2 2.0 %conditional.6 = (bf16[16,56,512]{2,1,0:T(8,128)(2,1)S(1)}) conditional(s32[]{:T(128)} %convert_element_type.191, () %tuple.59, (bf16[1024,512]{1,0:T(8,128)(2,1)}, bf16[896,512]{1,0:T(8,128)(2,1)}) %tuple.139), branch_computations={%region_35.36_spmd, %region_36.37_spmd} | conditional | flops 470220800 | bytes 2359304 | solution.py:498
  64.2 2.0 %convolution_convert_fusion.2 = bf16[896,512]{1,0:T(8,128)(2,1)S(1)} fusion(bf16[896,512]{1,0:T(8,128)(2,1)} %get-tuple-element.564, bf16[1024,512]{1,0:T(8,128)(2,1)} %get-tuple-element.565), kind=kOutput, calls=%fused_computation.11 | convolution fusion | flops 470220800 | bytes 2359296 | tf_op jit(solution)/shard_map/cond/branch_1_fun/dot_general | solution.py:433
  66.2 2.2 %convolution_convert_fusion.14 = bf16[96,512]{1,0:T(8,128)(2,1)} fusion(bf16[1024,512]{1,0:T(8,128)(2,1)} %bitcast.17, s32[96]{0:T(128)S(1)} %broadcast_add_fusion.9), kind=kOutput, calls=%fused_computation.130 | convolution fusion | flops 100810752 | bytes 1147264 | tf_op jit(solution)/shard_map/dot_general | solution.py:433
  68.4 59.7 %panel_spread_2.1 = (bf16[2,8,4,16,512]{4,3,2,1,0:T(8,128)(2,1)}, bf16[2,4,8,24,512]{4,3,2,1,0:T(8,128)(2,1)}, bf16[2,4,4,16,512]{4,3,2,1,0:T(8,128)(2,1)}, bf16...) custom-call(bf16[8,4,16,512]{3,2,1,0:T(8,128)(2,1)} %bitcast.129, bf16[4,8,24,512]{3,2,1,0:T(8,128)(2,1)} %bitcast.128, ...), custom_call_target="tpu_custom_call" | custom-call | tf_op jit(solution)/shard_map/panel_spread_2/pallas_call | solution.py:374
  128.1 2.5 %fusion.138 = (bf16[1,4,8,24,512]{4,3,2,1,0:T(8,128)(2,1)}, bf16[1,4,8,24,512]{4,3,2,1,0:T(8,128)(2,1)S(1)}) fusion(bf16[2,4,8,24,512]{4,3,2,1,0:T(8,128)(2,1)} %get-tuple-element.583), kind=kLoop, calls=%fused_computation.308 | loop fusion | bytes 3145728 | tf_op jit(solution)/shard_map/slice | solution.py:548
  130.6 0.7 convolution_convert_fusion.7
  131.3 0.5 copy-done.22
  131.8 0.4 convolution_convert_fusion.11
  132.3 1.7 subtract_convert_fusion.3
  134.0 1.2 bitcast_select_fusion.2
  135.2 0.8 copy-done.13
  136.0 0.2 copy-done.14
  136.2 1.6 convolution_convert_fusion.13
  137.8 0.4 fusion.48
  138.2 1.3 convolution_convert_fusion.10
  139.5 3.7 %subtract_convert_fusion.4 = bf16[1024,512]{1,0:T(8,128)(2,1)} fusion(bf16[1024,512]{1,0:T(8,128)(2,1)} %copy-done.25, bf16[768,512]{1,0:T(8,128)(2,1)S(1)} %bitcast.132, bf16[256,512]{1,0:T(8,128)(2,1)S(1)} %get-tuple-element.672, bf16[2,256,512]{2,1,0:T(8,128)(2,1)} %copy-done.14, bf16[2,256,512]{2,1,0:T(8,128)(2,1)} %copy-done.13, ...), kind=kOutput, calls=%fused_computation.102 | convolution fusion | flops 809762816 | bytes 4718592 | tf_op jit(solution)/shard_map/dot_general | solution.py:433
  143.1 3.1 %convolution_convert_fusion.6 = bf16[1024,512]{1,0:T(8,128)(2,1)} fusion(bf16[1024,512]{1,0:T(8,128)(2,1)} %subtract_convert_fusion.4, bf16[2,512,512]{2,1,0:T(8,128)(2,1)} %param.17), kind=kOutput, calls=%fused_computation.110 | convolution fusion | flops 537395200 | bytes 2621440 | tf_op jit(solution)/shard_map/dot_general | solution.py:433
  146.2 3.3 %fusion.51 = bf16[1024,512]{1,0:T(8,128)(2,1)S(1)} fusion(bf16[1024,512]{1,0:T(8,128)(2,1)} %copy-done.25, bf16[1024,512]{1,0:T(8,128)(2,1)} %convolution_convert_fusion.6, bf16[512,512]{0,1:T(8,128)(2,1)} %convolution_convert_fusion.10, bf16[1024,512]{1,0:T(8,128)(2,1)} %subtract_convert_fusion.3, pred[]{:T(512)S(6)} %eq.519, pred[]{:T(512)S(6)} %eq.467), kind=kOutput, calls=%fused_computation.129 | convolution fusion | flops 539492352 | bytes 4718594 | tf_op jit(solution)/shard_map/dot_general | solution.py:433
  149.5 1.2 fusion.70
  150.8 1.6 copy.13
  152.5 3.2 %fusion.50 = bf16[1024,512]{1,0:T(8,128)(2,1)S(1)} fusion(bf16[1024,512]{1,0:T(8,128)(2,1)} %get-tuple-element.585, bf16[1536,512]{1,0:T(8,128)(2,1)S(1)} %bitcast.160, s32[1024]{0:T(1024)S(1)} %get-tuple-element.676), kind=kOutput, calls=%fused_computation.128 | convolution fusion | flops 1613234176 | bytes 3674112 | tf_op jit(solution)/shard_map/dot_general | solution.py:433
  155.7 1.0 copy-done.28
  156.7 0.4 convolution_convert_fusion.9
  157.1 3.0 %convolution_convert_fusion.8 = bf16[512,512]{0,1:T(8,128)(2,1)} fusion(bf16[512,512]{1,0:T(8,128)(2,1)S(1)} %copy-done.8, bf16[512,512]{0,1:T(8,128)(2,1)S(1)} %convolution_convert_fusion.9, bf16[1024,512]{1,0:T(8,128)(2,1)} %copy-done.28, bf16[2,512,512]{2,1,0:T(8,128)(2,1)} %param.16), kind=kOutput, calls=%fused_computation.120 | convolution fusion | flops 537919488 | bytes 2621440 | tf_op jit(solution)/shard_map/dot_general | solution.py:433
  160.2 1.9 %fusion.47 = bf16[1024,512]{1,0:T(8,128)(2,1)S(1)} fusion(bf16[1024,512]{1,0:T(8,128)(2,1)} %get-tuple-element.587, bf16[112,512]{1,0:T(8,128)(2,1)S(1)} %bitcast.154, pred[1024]{0:T(1024)(128)(4,1)S(1)} %compare_reduce_fusion.8, s32[112]{0:T(128)S(1)} %broadcast_add_fusion.8), kind=kOutput, calls=%fused_computation.113 | convolution fusion | flops 118603776 | bytes 2213312 | tf_op jit(solution)/shard_map/dot_general | solution.py:433
  162.1 0.7 subtract_convert_fusion.1
  162.8 0.3 copy-done.17
  163.1 0.3 copy-done.27
  163.5 0.7 subtract_convert_fusion
  164.2 0.2 fusion.67
  164.5 1.9 %copy.14 = bf16[2,512,1,512]{3,2,1,0:T(2,128)(2,1)S(1)} copy(bf16[2,512,1,512]{3,1,0,2:T(8,128)(2,1)S(1)} %bitcast.125) | data formatting | bytes 2097152 | tf_op jit(solution)/shard_map/stack;reshape | solution.py:573
  166.4 5.6 %maximum_bitcast_fusion = bf16[2,1,512,2,1,512]{5,3,4,2,1,0:T(2,128)(2,1)} fusion(bf16[2,512,1,512]{3,2,1,0:T(2,128)(2,1)S(1)} %copy.14, bf16[2,512,1,512]{3,2,1,0:T(2,128)(2,1)S(1)} %copy.13), kind=kLoop, calls=%fused_computation.97 | loop fusion | flops 4194304 | bytes 4194304 | tf_op jit(solution)/shard_map/reshape | solution.py:573
  (72 shorter events, 0.9 us)
Async XLA Ops:
  7.4 6.8 %copy-start.5 = (bf16[896,512]{1,0:T(8,128)(2,1)}, bf16[896,512]{1,0:T(8,128)(2,1)S(1)}, u32[]{:S(2)}) copy-start(bf16[896,512]{1,0:T(8,128)(2,1)S(1)} %fusion.63) | copy-start | bytes 2752516
  48.1 1.9 %copy-start.20 = (bf16[16,2,48,512]{3,2,1,0:T(8,128)(2,1)S(1)}, bf16[16,2,48,512]{3,2,1,0:T(8,128)(2,1)}, u32[]{:S(2)}) copy-start(bf16[16,2,48,512]{3,2,1,0:T(8,128)(2,1)} %get-tuple-element.577) | copy-start | bytes 4718596
  128.0 2.5 %copy-start.4 = (bf16[2,8,4,16,512]{4,3,2,1,0:T(8,128)(2,1)S(1)}, bf16[2,8,4,16,512]{4,3,2,1,0:T(8,128)(2,1)}, u32[]{:S(2)}) copy-start(bf16[2,8,4,16,512]{4,3,2,1,0:T(8,128)(2,1)} %get-tuple-element.581) | copy-start | bytes 3145732
  128.0 2.6 %copy-start.21 = (bf16[2,512,512]{2,1,0:T(8,128)(2,1)S(1)}, bf16[2,512,512]{2,1,0:T(8,128)(2,1)}, u32[]{:S(2)}) copy-start(bf16[2,512,512]{2,1,0:T(8,128)(2,1)} %param.17) | copy-start | bytes 3145732
  130.6 1.2 copy-start.22
  131.8 2.2 %copy-start.25 = (bf16[1024,512]{1,0:T(8,128)(2,1)}, bf16[1024,512]{1,0:T(8,128)(2,1)S(1)}, u32[]{:S(2)}) copy-start(bf16[1024,512]{1,0:T(8,128)(2,1)S(1)} %convolution_convert_fusion.7) | copy-start | bytes 3145732
  132.3 1.7 copy-start.9
  134.0 3.7 %copy-start.10 = (bf16[512,512]{0,1:T(8,128)(2,1)S(1)}, bf16[512,512]{0,1:T(8,128)(2,1)}, u32[]{:S(2)}) copy-start(bf16[512,512]{0,1:T(8,128)(2,1)} %copy-done.9) | copy-start | bytes 1572868
  135.2 0.8 copy-start.13
  135.2 1.0 copy-start.14
  136.2 2.0 %copy-start.23 = (bf16[2,512,512]{2,1,0:T(8,128)(2,1)S(1)}, bf16[2,512,512]{2,1,0:T(8,128)(2,1)}, u32[]{:S(2)}) copy-start(bf16[2,512,512]{2,1,0:T(8,128)(2,1)} %param.16) | copy-start | bytes 3145732
  137.7 11.8 %copy-start.7 = (bf16[512,512]{1,0:T(8,128)(2,1)}, bf16[512,512]{1,0:T(8,128)(2,1)S(1)}, u32[]{:S(2)}) copy-start(bf16[512,512]{1,0:T(8,128)(2,1)S(1)} %convolution_convert_fusion.13) | copy-start | bytes 1572868
  137.8 1.7 %copy-start.6 = (bf16[1,4,8,24,512]{4,3,2,1,0:T(8,128)(2,1)S(1)}, bf16[1,4,8,24,512]{4,3,2,1,0:T(8,128)(2,1)}, u32[]{:S(2)}) copy-start(bf16[1,4,8,24,512]{4,3,2,1,0:T(8,128)(2,1)} %get-tuple-element.666) | copy-start | bytes 2359300
  138.2 4.9 %copy-start.12 = (bf16[512,512]{1,0:T(8,128)(2,1)}, bf16[512,512]{1,0:T(8,128)(2,1)S(1)}, u32[]{:S(2)}) copy-start(bf16[512,512]{1,0:T(8,128)(2,1)S(1)} %fusion.48) | copy-start | bytes 1572868
  146.2 3.3 %copy-start.11 = (bf16[512,512]{0,1:T(8,128)(2,1)S(1)}, bf16[512,512]{0,1:T(8,128)(2,1)}, u32[]{:S(2)}) copy-start(bf16[512,512]{0,1:T(8,128)(2,1)} %copy-done.9) | copy-start | bytes 1572868
  150.8 1.6 copy-start.19
  152.5 4.2 %copy-start.24 = (bf16[2,512,512]{2,1,0:T(8,128)(2,1)S(1)}, bf16[2,512,512]{2,1,0:T(8,128)(2,1)}, u32[]{:S(2)}) copy-start(bf16[2,512,512]{2,1,0:T(8,128)(2,1)} %param.16) | copy-start | bytes 3145732
  152.5 4.6 %copy-start.8 = (bf16[512,512]{1,0:T(8,128)(2,1)S(1)}, bf16[512,512]{1,0:T(8,128)(2,1)}, u32[]{:S(2)}) copy-start(bf16[512,512]{1,0:T(8,128)(2,1)} %copy-done.7) | copy-start | bytes 1572868
  155.7 1.0 copy-start.28
  157.1 3.0 %copy-start.15 = (bf16[512,512]{0,1:T(8,128)(2,1)}, bf16[512,512]{0,1:T(8,128)(2,1)S(1)}, u32[]{:S(2)}) copy-start(bf16[512,512]{0,1:T(8,128)(2,1)S(1)} %convolution_convert_fusion.9) | copy-start | bytes 1572868
  157.1 3.0 %copy-start.18 = (bf16[2,56,512]{2,1,0:T(8,128)(2,1)S(1)}, bf16[2,56,512]{2,1,0:T(8,128)(2,1)}, u32[]{:S(2)}) copy-start(bf16[2,56,512]{2,1,0:T(8,128)(2,1)} %get-tuple-element.586) | copy-start | bytes 344068
  160.1 1.9 %copy-start.26 = (bf16[1024,512]{1,0:T(8,128)(2,1)S(1)}, bf16[1024,512]{1,0:T(8,128)(2,1)}, u32[]{:S(2)}) copy-start(bf16[1024,512]{1,0:T(8,128)(2,1)} %copy-done.25) | copy-start | bytes 3145732
  160.1 1.9 %copy-start.16 = (bf16[512,512]{0,1:T(8,128)(2,1)S(1)}, bf16[512,512]{0,1:T(8,128)(2,1)}, u32[]{:S(2)}) copy-start(bf16[512,512]{0,1:T(8,128)(2,1)} %copy-done.15) | copy-start | bytes 1572868
  162.1 1.0 copy-start.17
  162.1 1.4 copy-start.27

commit v2 on v1

--- a/solution.py
+++ b/solution.py
@@ -10,8 +10,10 @@
 NX = 4
 CAP = 96
 DCAP = 56
-PA = 16
-PB = 24
+MOVED = CORES * DCAP
+HALF = NB // CORES
+PA = 32
+PB = 16
 MESH = pl.DeviceIdType.MESH
 ANY = pl.BlockSpec(memory_space=pl.ANY)
 
@@ -246,29 +248,16 @@
         out_specs=(ANY, ANY),
         scratch_shapes=exchange_sems(ny),
         compiler_params=pltpu.CompilerParams(collective_id=cid, has_side_effects=True),
-        name="row_exchange_%d" % cid,
+        name="row_exchange",
     )(sent, spread)
 
 
-def spread_kernel(ny, nz, nexch, *refs):
-    src_a, src_b, sent, spread, buf_a, buf_b, other, rows, moved = refs[:9]
-    sems = refs[9 : 9 + nexch]
-    (axs, axr, azs, azr, bzs, bzr, bxs, bxr, ss, sr, ts, tr) = refs[9 + nexch :]
-    ex = RowExchange(ny, sent, spread, rows, moved, sems)
-    pcol = lax.axis_index("pcol")
-    n = nz * NX
-    z, x = lax.div(pcol, NX), lax.rem(pcol, NX)
-
+def meet_with_roots(near, pcol, n):
     barrier = pltpu.get_barrier_semaphore()
 
     def signal(peer):
         pl.semaphore_signal(barrier, inc=1, device_id=peer, device_id_type=MESH)
 
-    near = ex.barrier_peers()
-    near += [{"pcol": z * NX + lax.rem(x + d, NX)} for d in (1, NX - 1)]
-    near += [{"pcol": lax.rem(z + d, nz) * NX + x} for d in (1, nz - 1)]
-    for peer in near:
-        signal(peer)
     for root in (0, 1):
         @pl.when(pcol == root)
         def _():
@@ -279,6 +268,9 @@
         def _():
             signal({"pcol": root})
 
+    for peer in near:
+        signal(peer)
+
     @pl.when(pcol < 2)
     def _():
         pl.semaphore_wait(barrier, len(near) + n)
@@ -287,26 +279,111 @@
     def _():
         pl.semaphore_wait(barrier, len(near) + 2)
 
-    def scatter_copies(k):
-        to = lax.rem(pcol + k, n)
-        tz, tx = lax.div(to, NX), lax.rem(to, NX)
-        args = dict(device_id={"pcol": to}, device_id_type=MESH)
-        a = pltpu.make_async_remote_copy(
-            src_ref=src_a.at[tz, tx], dst_ref=buf_a.at[pcol, tz, tx],
-            send_sem=ss.at[k, 0], recv_sem=sr.at[0, pcol], **args)
-        b = pltpu.make_async_remote_copy(
-            src_ref=src_b.at[tx, tz], dst_ref=buf_b.at[pcol, tx, tz],
-            send_sem=ss.at[k, 1], recv_sem=sr.at[1, pcol], **args)
-        return a, b
-
-    def scatter():
-        @pl.when(pcol < 2)
+
+class Scatter:
+    def __init__(self, pcol, n, piece, slot, send, recv):
+        self.pcol, self.n, self.piece, self.slot, self.send, self.recv = pcol, n, piece, slot, send, recv
+
+    def copy(self, k):
+        to = lax.rem(self.pcol + k, self.n)
+        return pltpu.make_async_remote_copy(
+            src_ref=self.piece(to), dst_ref=self.slot(self.pcol, to),
+            send_sem=self.send.at[k], recv_sem=self.recv.at[self.pcol],
+            device_id={"pcol": to}, device_id_type=MESH)
+
+    def start(self):
+        @pl.when(self.pcol < 2)
         def _():
-            for which in (0, 1):
-                for k in range(1, n):
-                    scatter_copies(k)[which].start()
-            pltpu.make_async_copy(src_a.at[z, x], buf_a.at[pcol, z, x], sr.at[0, pcol]).start()
-            pltpu.make_async_copy(src_b.at[x, z], buf_b.at[pcol, x, z], sr.at[1, pcol]).start()
+            for k in range(1, self.n):
+                self.copy(k).start()
+            pltpu.make_async_copy(
+                self.piece(self.pcol), self.slot(self.pcol, self.pcol), self.recv.at[self.pcol]
+            ).start()
+
+    def landed(self, panel):
+        ref = self.slot(panel, self.pcol)
+        pltpu.make_async_copy(ref, ref, self.recv.at[panel]).wait()
+
+    def drain(self):
+        @pl.when(self.pcol < 2)
+        def _():
+            for k in range(1, self.n):
+                self.copy(k).wait_send()
+
+
+def first_kernel(ny, nz, nexch, *refs):
+    tile, sent, spread, piece, rows, moved = refs[:6]
+    ex = RowExchange(ny, sent, spread, rows, moved, refs[6 : 6 + nexch])
+    ss, sr = refs[6 + nexch :]
+    pcol = lax.axis_index("pcol")
+    n = nz * NX
+    scatter = Scatter(
+        pcol, n,
+        lambda to: tile.at[pl.ds(pl.multiple_of(to * PA, PA), PA), pl.ds(0, NB)],
+        lambda panel, to: piece.at[panel], ss, sr)
+    meet_with_roots(ex.barrier_peers(), pcol, n)
+    run_events(ex.events(3.8) + [(0.0, scatter.start)])
+    ex.finish()
+    for panel in (0, 1):
+        scatter.landed(panel)
+    scatter.drain()
+
+
+def first_exchange(tile, sent, spread, ny, nz, cid):
+    width = sent.shape[-1]
+    sems = exchange_sems(ny)
+    dma = pltpu.SemaphoreType.DMA
+    return pl.pallas_call(
+        lambda *refs: first_kernel(ny, nz, len(sems), *refs),
+        out_shape=(
+            jax.ShapeDtypeStruct((2, PA, NB), jnp.bfloat16),
+            jax.ShapeDtypeStruct((ny * CORES, 2, CAP // 2, width), jnp.bfloat16),
+            jax.ShapeDtypeStruct((CORES, DCAP, width), jnp.bfloat16),
+        ),
+        in_specs=[ANY] * 3,
+        out_specs=(ANY,) * 3,
+        scratch_shapes=sems + [dma((nz * NX,)), dma((2,))],
+        compiler_params=pltpu.CompilerParams(collective_id=cid, has_side_effects=True),
+        name="first_exchange",
+    )(tile, sent, spread)
+
+
+class Direct:
+    def __init__(self, n, pos, goto, item, fresh, send, recv):
+        self.n, self.pos, self.goto, self.item, self.fresh, self.send, self.recv = n, pos, goto, item, fresh, send, recv
+
+    def copy(self, k, half):
+        to = lax.rem(self.pos + k, self.n)
+        return pltpu.make_async_remote_copy(
+            src_ref=self.fresh(half), dst_ref=self.item(self.pos, half),
+            send_sem=self.send.at[k, half], recv_sem=self.recv.at[k, half],
+            device_id=self.goto(to), device_id_type=MESH)
+
+    def start(self):
+        for half in (0, 1):
+            for k in range(1, self.n):
+                self.copy(k, half).start()
+            pltpu.make_async_copy(
+                self.fresh(half), self.item(self.pos, half), self.recv.at[0, half]).start()
+
+    def wait(self, half):
+        for k in range(self.n):
+            ref = self.item(lax.rem(self.pos + self.n - k, self.n), half)
+            pltpu.make_async_copy(ref, ref, self.recv.at[k, half]).wait()
+
+    def drain(self):
+        for half in (0, 1):
+            for k in range(1, self.n):
+                self.copy(k, half).wait_send()
+
+
+def second_kernel(ny, nz, nexch, *refs):
+    piece, small, sent, spread, raw, extra, other, rows, moved = refs[:9]
+    ex = RowExchange(ny, sent, spread, rows, moved, refs[9 : 9 + nexch])
+    (axs, axr, azs, azr, bzs, bzr, bxs, bxr, ss, sr, ts, tr, to_s, to_r) = refs[9 + nexch :]
+    pcol = lax.axis_index("pcol")
+    n = nz * NX
+    z, x = lax.div(pcol, NX), lax.rem(pcol, NX)
 
     def to_x(i):
         return {"pcol": z * NX + i}
@@ -314,81 +391,351 @@
     def to_z(i):
         return {"pcol": i * NX + x}
 
-    ax = Ring(NX, x, to_x, lambda i, h: buf_a.at[h, z, i], axs, axr)
-    az = Ring(nz, z, to_z, lambda i, h: buf_a.at[h, i], azs, azr)
-    bz = Ring(nz, z, to_z, lambda i, h: buf_b.at[h, x, i], bzs, bzr)
-    bx = Ring(NX, x, to_x, lambda i, h: buf_b.at[h, i], bxs, bxr)
-
-    def own(which, half):
-        ref = buf_a.at[half, z, x] if which == 0 else buf_b.at[half, x, z]
-        pltpu.make_async_copy(ref, ref, sr.at[which, half]).wait()
-
-    def begin(ring, half, which=None, after=None):
-        if which is not None:
-            own(which, half)
-        if after is not None:
-            after.complete(half)
-        ring.start(half)
-
-    def across(half):
+    near = ex.barrier_peers()
+    near += [to_x(lax.rem(x + d, NX)) for d in range(1, NX)]
+    near += [to_z(lax.rem(z + d, nz)) for d in (1, nz - 1)]
+    meet_with_roots(near, pcol, n)
+
+    tops = nz // 2
+
+    def across(index, way, hop, half, sems=None):
+        s, r = (ts.at[way, hop - 1, half], tr.at[way, hop - 1, half]) if hop else (to_s.at[half], to_r.at[half])
         return pltpu.make_async_remote_copy(
-            src_ref=buf_a.at[half, pl.ds(0, nz // 2)], dst_ref=other.at[half],
-            send_sem=ts.at[half], recv_sem=tr.at[half],
-            device_id=ex.partner, device_id_type=MESH)
-
-    def send_other(half):
-        az.complete(half)
-        across(half).start()
-
-    events = [(-0.5, scatter)]
-    events += ex.events(3.8)
-    events += [(5.0 + h * 0.1, lambda h=h: begin(ax, h, which=0)) for h in (0, 1)]
-    events += ax.events([5.0, 5.2], 1.8)
-    events += [(7.0 + h * 0.1, lambda h=h: begin(bz, h, which=1)) for h in (0, 1)]
-    events += bz.events([7.2, 7.4], 2.2)
-    events += [(9.0 + h * 0.1, lambda h=h: begin(az, h, after=ax)) for h in (0, 1)]
-    events += az.events([9.2, 9.5], 3.4)
-    events += [(16.5 + h * 0.1, lambda h=h: begin(bx, h, after=bz)) for h in (0, 1)]
-    events += bx.events([17.0, 18.0], 6.0)
-    events += [(25.0 + h * 0.1, lambda h=h: send_other(h)) for h in (0, 1)]
+            src_ref=extra.at[half, index, pl.ds(0, tops)], dst_ref=other.at[half, index],
+            send_sem=s, recv_sem=r, device_id=ex.partner, device_id_type=MESH)
+
+    crossing = []
+
+    def cross(index, ref, way, hop, half):
+        copy = across(index, way, hop, half)
+        copy.start()
+        crossing.append(copy)
+
+    scatter = Scatter(
+        pcol, n,
+        lambda to: small.at[lax.rem(to, NX), lax.div(to, NX)],
+        lambda panel, to: extra.at[panel, lax.rem(to, NX), lax.div(to, NX)], ss, sr)
+    ax = Direct(NX, x, to_x, lambda i, h: raw.at[h, z, i], lambda h: piece.at[h], axs, axr)
+    az = Ring(nz, z, to_z, lambda i, h: raw.at[h, i], azs, azr)
+    bz = Ring(nz, z, to_z, lambda i, h: extra.at[h, x, i], bzs, bzr)
+    bx = Ring(NX, x, to_x, lambda i, h: extra.at[h, i], bxs, bxr, arrived=cross)
+
+    def begin_az(half):
+        ax.wait(half)
+        az.start(half)
+
+    def begin_bz(half):
+        scatter.landed(half)
+        bz.start(half)
+
+    def begin_bx(half):
+        bz.complete(half)
+        bx.start(half)
+        cross(x, None, 0, 0, half)
+
+    events = [(-0.6, scatter.start), (-0.5, ax.start)]
+    events += ex.events(4.5)
+    events += [(3.5 + h * 0.3, lambda h=h: begin_az(h)) for h in (0, 1)]
+    events += az.events([3.5, 5.5], 5.0)
+    events += [(5.0 + h * 0.1, lambda h=h: begin_bz(h)) for h in (0, 1)]
+    events += bz.events([5.2, 5.4], 3.0)
+    events += [(17.6 + h * 0.1, lambda h=h: begin_bx(h)) for h in (0, 1)]
+    events += bx.events([18.0, 19.5], 3.5)
     run_events(events)
     ex.finish()
-    for ring in (ax, az, bz, bx):
+    for ring in (az, bz, bx):
         for half in (0, 1):
             ring.complete(half)
         ring.drain()
-    for half in (0, 1):
-        across(half).wait()
-
-    @pl.when(pcol < 2)
-    def _():
-        for k in range(1, n):
-            for copy in scatter_copies(k):
-                copy.wait_send()
-
-
-def panel_spread(src_a, src_b, sent, spread, ny, nz, cid):
+    ax.drain()
+    scatter.drain()
+    for copy in crossing:
+        copy.wait()
+
+
+def second_exchange(piece, small, sent, spread, ny, nz, cid):
     width = sent.shape[-1]
     dma = pltpu.SemaphoreType.DMA
     sems = exchange_sems(ny)
+    zring, xring = dma((2, nz // 2, 2)), dma((2, NX // 2, 2))
+    direct = dma((NX, 2))
     return pl.pallas_call(
-        lambda *refs: spread_kernel(ny, nz, len(sems), *refs),
+        lambda *refs: second_kernel(ny, nz, len(sems), *refs),
         out_shape=(
             jax.ShapeDtypeStruct((2, nz, NX, PA, NB), jnp.bfloat16),
             jax.ShapeDtypeStruct((2, NX, nz, PB, NB), jnp.bfloat16),
-            jax.ShapeDtypeStruct((2, nz // 2, NX, PA, NB), jnp.bfloat16),
+            jax.ShapeDtypeStruct((2, NX, nz // 2, PB, NB), jnp.bfloat16),
             jax.ShapeDtypeStruct((ny * CORES, 2, CAP // 2, width), jnp.bfloat16),
             jax.ShapeDtypeStruct((CORES, DCAP, width), jnp.bfloat16),
         ),
         in_specs=[ANY] * 4,
         out_specs=(ANY,) * 5,
         scratch_shapes=sems
-        + [dma((2, NX // 2, 2)), dma((2, NX // 2, 2)), dma((2, nz // 2, 2)), dma((2, nz // 2, 2))]
-        + [dma((2, nz // 2, 2)), dma((2, nz // 2, 2)), dma((2, NX // 2, 2)), dma((2, NX // 2, 2))]
-        + [dma((nz * NX, 2)), dma((2, 2)), dma((2,)), dma((2,))],
+        + [direct, direct, zring, zring, zring, zring, xring, xring]
+        + [dma((nz * NX,)), dma((2,)), xring, xring, dma((2,)), dma((2,))],
         compiler_params=pltpu.CompilerParams(collective_id=cid, has_side_effects=True),
-        name="panel_spread_%d" % cid,
-    )(src_a, src_b, sent, spread)
+        name="second_exchange",
+    )(piece, small, sent, spread)
+
+
+def dot(a, b):
+    return jnp.dot(a, b, preferred_element_type=jnp.float32)
+
+
+def bdot(a, b):
+    return dot(a, b).astype(jnp.bfloat16)
+
+
+def ids(shape, axis):
+    return lax.broadcasted_iota(jnp.int32, shape, axis).astype(jnp.float32)
+
+
+def to_row(col):
+    n = col.shape[0]
+    return jnp.sum(jnp.where(ids((n, n), 0) == ids((n, n), 1), col, 0.0), axis=0, keepdims=True)
+
+
+def to_col(row):
+    n = row.shape[1]
+    return jnp.sum(jnp.where(ids((n, n), 0) == ids((n, n), 1), row, 0.0), axis=1, keepdims=True)
+
+
+def along(table):
+    return jnp.sum(table, axis=1, keepdims=True)
+
+
+def down(table):
+    return jnp.sum(table, axis=0, keepdims=True)
+
+
+def hot(mask):
+    return jnp.where(mask, 1.0, 0.0).astype(jnp.bfloat16)
+
+
+def index_kernel(nprow, piv, tile, sent0, sent1, spread0, spread1, slot_out, into_out, rounds_out):
+    prow = lax.axis_index("prow")
+    core = lax.rem(prow, CORES).astype(jnp.float32)
+    prow_f = prow.astype(jnp.float32)
+    rows = [piv[k : k + 1, :].astype(jnp.float32) for k in (0, 1)]
+    cols = [to_col(r) for r in rows]
+    i0, i1 = ids((NB, NB), 0), ids((NB, NB), 1)
+    receive = []
+    for k in (0, 1):
+        first = float(k * NB)
+        top_c, top_r = ids((NB, 1), 0) + first, ids((1, NB), 1) + first
+        left_c = 1.0 - along(jnp.where(rows[k] == top_c, 1.0, 0.0))
+        left_r = 1.0 - down(jnp.where(cols[k] == top_r, 1.0, 0.0))
+        rank_r = down(jnp.where(i0 < i1, left_c, 0.0))
+        vac_r = jnp.where(rows[k] >= first + NB, 1.0, 0.0)
+        vac_c = along(jnp.where(i1 < i0, vac_r, 0.0))
+        receive.append(along(jnp.where((rank_r == vac_c) & (left_r > 0.5), top_r, 0.0)))
+    receive0_r = to_row(receive[0])
+
+    def lookup(keys):
+        hit = keys == rows[0]
+        found = along(jnp.where(hit, 1.0, 0.0))
+        return jnp.where(found > 0.5, along(jnp.where(hit, receive0_r, 0.0)), keys)
+
+    src1, from1 = lookup(cols[1]), lookup(receive[1])
+    again = along(jnp.where(cols[0] == rows[1], 1.0, 0.0))
+
+    def owner(v):
+        return (lax.shift_right_logical(v.astype(jnp.int32), 9) & (nprow - 1)).astype(jnp.float32)
+
+    def local(v):
+        v = v.astype(jnp.int32)
+        return (lax.shift_right_logical(v, 13) * NB + (v & (NB - 1))).astype(jnp.float32)
+
+    n = 2 * NB
+    e0, e1 = ids((n, n), 0), ids((n, n), 1)
+
+    def rank(group_c):
+        group_r = to_row(group_c)
+        same = group_c == group_r
+        rank_c = along(jnp.where(same & (e1 < e0), 1.0, 0.0))
+        rank_r = down(jnp.where(same & (e0 < e1), 1.0, 0.0))
+        return group_r, rank_c, rank_r
+
+    t_c = jnp.concatenate([cols[0], src1], axis=0)
+    t_group = owner(t_c)
+    t_group_r, t_rank_c, t_rank_r = rank(t_group)
+    slot_c = jnp.where(t_rank_c < CAP, t_group * CAP + t_rank_c, -1.0)
+    slot_r = jnp.where(t_rank_r < CAP, t_group_r * CAP + t_rank_r, -1.0)
+    slot_out[...] = slot_c.astype(jnp.int32)
+    mine = ids((CAP, 1), 0) + prow_f * CAP
+    pick = along(jnp.where(slot_r == mine, local(to_row(t_c)) + 1.0, 0.0)) - 1.0
+    sent = bdot(hot(pick == ids((CAP, n), 1)), tile[...])
+    sent0[...] = sent[:, :NB]
+    sent1[...] = sent[:, NB:]
+
+    d_dst = jnp.concatenate([cols[0], cols[1]], axis=0)
+    d_src = jnp.concatenate([receive[0], from1], axis=0)
+    fresh = jnp.concatenate([again, jnp.zeros_like(again)], axis=0)
+    valid = (d_dst >= 2.0 * NB) & (fresh < 0.5)
+    group = jnp.where(valid, owner(d_dst) * CORES + jnp.where(d_src >= NB, 1.0, 0.0), -1.0)
+    group_r, rank_c, rank_r = rank(group)
+    key_c = jnp.where(valid & (rank_c < DCAP), group * DCAP + rank_c, -1.0)
+    lane = ids((1, 128), 1)
+    wanted = jnp.where(lane < MOVED, lane + prow_f * MOVED, -2.0)
+    into = down(jnp.where(key_c == wanted, local(d_dst) + 1.0, 0.0)) - 1.0
+    into_out[...] = into.astype(jnp.int32)
+    most_t = jnp.max(t_rank_c) * (1.0 / CAP)
+    most_d = jnp.max(jnp.where(valid, rank_c, 0.0)) * (1.0 / DCAP)
+    rounds_out[0, 0] = jnp.where(jnp.maximum(most_t, most_d) > 1.0 - 0.25 / CAP, 2, 1).astype(jnp.int32)
+
+    @pl.when(prow < CORES)
+    def _():
+        key_r = jnp.where((group_r > -0.5) & (rank_r < DCAP), group_r * DCAP + rank_r, -1.0)
+        src_r = to_row(d_src)
+        s = ids((MOVED, 1), 0)
+
+        def one_chip(q, _):
+            second = jnp.where(s >= DCAP, 1.0, 0.0)
+            want = (2.0 * q.astype(jnp.float32) + second) * MOVED + core * DCAP + s - second * DCAP
+            src = along(jnp.where(key_r == want, src_r + 1.0, 0.0)) - 1.0 - core * NB
+            out = bdot(hot(src == ids((MOVED, NB), 1)), tile[:NB, :])
+            here = pl.ds(pl.multiple_of(q * MOVED, MOVED), MOVED)
+            spread0[here, :] = out[:, :NB]
+            spread1[here, :] = out[:, NB:]
+            return 0
+
+        lax.fori_loop(0, nprow // 2, one_chip, 0)
+
+
+def index_and_pack(pivots, tile, nprow):
+    n = 2 * NB
+    bf16 = jnp.bfloat16
+    vmem = pl.BlockSpec(memory_space=pltpu.VMEM)
+    return pl.pallas_call(
+        lambda *refs: index_kernel(nprow, *refs),
+        out_shape=(
+            jax.ShapeDtypeStruct((CAP, NB), bf16), jax.ShapeDtypeStruct((CAP, NB), bf16),
+            jax.ShapeDtypeStruct((nprow * DCAP, NB), bf16), jax.ShapeDtypeStruct((nprow * DCAP, NB), bf16),
+            jax.ShapeDtypeStruct((n, 1), jnp.int32), jax.ShapeDtypeStruct((1, 128), jnp.int32),
+            jax.ShapeDtypeStruct((1, 1), jnp.int32),
+        ),
+        in_specs=[vmem, vmem],
+        out_specs=(vmem,) * 6 + (pl.BlockSpec(memory_space=pltpu.SMEM),),
+        name="index_and_pack",
+    )(pivots, tile)
+
+
+def panel_tops_kernel(rows, moved, slot, small):
+    pcol, prow = lax.axis_index("pcol"), lax.axis_index("prow")
+    first = jnp.where(pcol == 0, NB, 0) + lax.rem(prow, CORES) * HALF
+    first = pl.multiple_of(first, HALF)
+    keys = slot[pl.ds(first, HALF), :]
+    total = rows.shape[0]
+    place = jnp.where(keys == lax.broadcasted_iota(jnp.int32, (HALF, total), 1), 1.0, 0.0).astype(jnp.bfloat16)
+    part = bdot(place, rows[...])
+    step = HALF // NX
+    for x in range(NX):
+        small[x, pl.ds(0, step), :] = part[x * step : (x + 1) * step]
+    small[0, pl.ds(step, step), :] = moved[pl.ds(0, step), :]
+    small[1, pl.ds(step, MOVED - step), :] = moved[pl.ds(step, MOVED - step), :]
+    for x, start in ((1, MOVED), (2, step), (3, step)):
+        size = 2 * step - start if x > 1 else 2 * step - MOVED
+        small[x, pl.ds(2 * step - size, size), :] = jnp.zeros((size, NB), jnp.bfloat16)
+
+
+def panel_tops(rows, moved, slot, nz):
+    vmem = pl.BlockSpec(memory_space=pltpu.VMEM)
+    return pl.pallas_call(
+        panel_tops_kernel,
+        out_shape=jax.ShapeDtypeStruct((NX, nz * PB, NB), jnp.bfloat16),
+        in_specs=[vmem] * 3,
+        out_specs=vmem,
+        name="panel_tops",
+    )(rows, moved, slot)
+
+
+def update_kernel(raw, extra, other, rows0, rows1, moved0, moved1, slot, into, tile, low_inv, up_inv,
+                  out, top, low, up0, up1):
+    pcol, prow = lax.axis_index("pcol"), lax.axis_index("prow")
+    core = lax.rem(prow, CORES)
+    f32 = jnp.float32
+    step = NB // 2
+    halves = (pl.ds(0, NB), pl.ds(NB, NB))
+    total = rows0.shape[0]
+
+    def spot(i):
+        return pl.ds(pl.multiple_of(i * step, step), step)
+
+    def place_rows(i, _):
+        keys = slot[spot(i), :]
+        place = jnp.where(keys == lax.broadcasted_iota(jnp.int32, (step, total), 1), 1.0, 0.0).astype(jnp.bfloat16)
+        top[spot(i), halves[0]] = bdot(place, rows0[...])
+        top[spot(i), halves[1]] = bdot(place, rows1[...])
+        return 0
+
+    lax.fori_loop(0, 4, place_rows, 0)
+    l0, l1, u0, u1 = low_inv[0], low_inv[1], up_inv[0], up_inv[1]
+    panel_tops = []
+    half = HALF // NX
+    for k in (0, 1):
+        own = jnp.concatenate([extra[k, x, :half, :] for x in range(NX)], axis=0)
+        far = jnp.concatenate([other[k, x] for x in range(NX)], axis=0)
+        panel_tops.append(jnp.concatenate(
+            [jnp.where(core == 0, own, far), jnp.where(core == 0, far, own)], axis=0))
+    corner = bdot(panel_tops[0], u0)
+    upper = bdot(l0, panel_tops[1])
+    moved_panel = [
+        jnp.concatenate([extra[k, 0, half:, :], extra[k, 1, half : half + MOVED - half, :]], axis=0) for k in (0, 1)
+    ]
+    for cols in halves:
+        up0[:, cols] = bdot(l0, top[pl.ds(0, NB), cols])
+        low[:, cols] = (top[pl.ds(NB, NB), cols].astype(f32) - dot(corner, up0[:, cols])).astype(jnp.bfloat16)
+        up1[:, cols] = bdot(l1, low[:, cols])
+
+    def update(i, _):
+        here = spot(i)
+        ids_c = lax.broadcasted_iota(jnp.int32, (step, MOVED), 0) + i * step
+        match = jnp.where(ids_c == into[:, :MOVED], 1.0, 0.0)
+        hit = jnp.max(match, axis=1, keepdims=True) > 0.5
+        insert = match.astype(jnp.bfloat16)
+
+        def with_moved(new, old):
+            return jnp.where(hit, dot(insert, new), old.astype(f32)).astype(jnp.bfloat16)
+
+        factor0 = bdot(with_moved(moved_panel[0], raw[0, here, :]), u0)
+        panel1 = (with_moved(moved_panel[1], raw[1, here, :]).astype(f32) - dot(factor0, upper)).astype(jnp.bfloat16)
+        factor1 = bdot(panel1, u1)
+        for d, (cols, moved) in enumerate(zip(halves, (moved0, moved1))):
+            new = with_moved(moved[...], tile[here, cols]).astype(f32)
+            new = (new - dot(factor0, up0[:, cols])).astype(jnp.bfloat16).astype(f32)
+            new = (new - dot(factor1, up1[:, cols])).astype(jnp.bfloat16)
+            if d == 0:
+                new = jnp.where(pcol == 0, factor0, jnp.where(pcol == 1, factor1, new))
+            out[here, cols] = new
+        return 0
+
+    lax.fori_loop(0, 4, update, 0)
+    heads = pl.ds(0, NB)
+
+    @pl.when(prow == 0)
+    def _():
+        out[heads, halves[0]] = jnp.where(pcol == 0, top[heads, halves[0]], up0[:, halves[0]])
+        out[heads, halves[1]] = up0[:, halves[1]]
+
+    @pl.when(prow == 1)
+    def _():
+        out[heads, halves[0]] = jnp.where(
+            pcol == 0, corner, jnp.where(pcol == 1, low[:, halves[0]], up1[:, halves[0]]))
+        out[heads, halves[1]] = up1[:, halves[1]]
+
+
+def update(*args):
+    n = 2 * NB
+    vmem = pl.BlockSpec(memory_space=pltpu.VMEM)
+    bf16 = jnp.bfloat16
+    return pl.pallas_call(
+        update_kernel,
+        out_shape=jax.ShapeDtypeStruct((n, n), bf16),
+        in_specs=[vmem] * len(args),
+        out_specs=vmem,
+        scratch_shapes=[pltpu.VMEM((n, n), bf16)] + [pltpu.VMEM((NB, n), bf16)] * 3,
+        name="update",
+    )(*args)
 
 
 def count_before(flags):
@@ -429,21 +776,9 @@
     return (index[:, None] == jnp.arange(n, dtype=jnp.int32)[None, :]).astype(jnp.bfloat16)
 
 
-def dot(a, b):
-    return jnp.dot(a, b, preferred_element_type=jnp.float32)
-
-
-def bdot(a, b):
-    return dot(a, b).astype(jnp.bfloat16)
-
-
-def per_device(matrix, pivots, lower_inverse, upper_inverse):
-    nprow, npcol = lax.axis_size("prow"), lax.axis_size("pcol")
-    ny, nz = nprow // CORES, npcol // NX
-    prow, pcol = lax.axis_index("prow"), lax.axis_index("pcol")
+def collect_rounds(tile, pivots, nprow, ny):
+    prow = lax.axis_index("prow")
     core = lax.rem(prow, CORES)
-    tiles = [matrix[:, 0, :, d, 0, :].reshape(2 * NB, NB) for d in (0, 1)]
-
     s0, s1 = pivots[0], pivots[1]
     receive0, receive1 = pairing(s0, 0), pairing(s1, NB)
     src1 = lookup(s1, s0, receive0)
@@ -468,109 +803,70 @@
     d_owner = owner(d_dst)
     d_rank = rank_in(jnp.where(d_valid, d_owner * CORES + d_core, -1))
     d_local = local(d_dst)
-    rounds = jnp.maximum(
-        jnp.max(t_rank) // CAP, jnp.max(jnp.where(d_valid, d_rank, 0)) // DCAP
-    ) + 1
-
-    def plan(r):
+    rounds = jnp.maximum(jnp.max(t_rank) // CAP, jnp.max(jnp.where(d_valid, d_rank, 0)) // DCAP) + 1
+
+    def body(state):
+        r, top, now = state
         t_in = (t_rank // CAP) == r
         t_slot = t_owner * CAP + lax.rem(t_rank, CAP)
+        t_key = jnp.where(t_in, t_slot, big)
         d_in = d_valid & ((d_rank // DCAP) == r)
-        d_slot = (d_owner * CORES + d_core) * DCAP + lax.rem(d_rank, DCAP)
-        t_key = jnp.where(t_in, t_slot, big)
-        d_key = jnp.where(d_in, d_slot, big)
-        send_sel = one_hot(slot_values(t_key, t_local, prow * CAP + jnp.arange(CAP, dtype=jnp.int32)), 2 * NB)
-        place = one_hot(jnp.where(t_in, t_slot, -1), nprow * CAP)
+        d_key = jnp.where(d_in, (d_owner * CORES + d_core) * DCAP + lax.rem(d_rank, DCAP), big)
+        pick = one_hot(slot_values(t_key, t_local, prow * CAP + jnp.arange(CAP, dtype=jnp.int32)), 2 * NB)
         every = jnp.arange(nprow * DCAP, dtype=jnp.int32)
         wanted = (every // DCAP * CORES + core) * DCAP + lax.rem(every, DCAP)
-        spread_sel = one_hot(lax.rem(slot_values(d_key, d_src + NB, wanted), NB + 0) * 1, NB)
-        have = slot_values(d_key, d_src, wanted) >= 0
-        spread_sel = jnp.where(have[:, None], spread_sel, jnp.zeros_like(spread_sel))
-        mine = prow * CORES * DCAP + jnp.arange(CORES * DCAP, dtype=jnp.int32)
+        spread_sel = one_hot(slot_values(d_key, d_src - core * NB, wanted), NB)
+        mine = prow * MOVED + jnp.arange(MOVED, dtype=jnp.int32)
         into = slot_values(d_key, d_local, mine)
         insert = (jnp.arange(2 * NB, dtype=jnp.int32)[:, None] == into[None, :]).astype(jnp.bfloat16)
-        hit = jnp.any(insert > 0, axis=1)
-        return send_sel, place, spread_sel, insert, hit
-
-    def pack(sel, spread_sel, tile):
-        width = tile.shape[1]
-        sent = bdot(sel, tile).reshape(2, CAP // 2, width)
-        spread = lax.cond(
-            prow < CORES,
-            lambda: bdot(spread_sel, tile[:NB]),
-            lambda: jnp.zeros((nprow * DCAP, width), jnp.bfloat16),
-        ).reshape(nprow, DCAP, width)
-        return sent, spread
-
-    def unpack_rows(place, rows):
-        return bdot(place, rows.reshape(nprow * CAP, rows.shape[-1]))
-
-    def unpack_moved(insert, hit, moved, tile):
-        new = bdot(insert, moved.reshape(CORES * DCAP, moved.shape[-1]))
-        return jnp.where(hit[:, None], new, tile)
-
-    send_sel, place, spread_sel, insert, hit = plan(0)
-    packs = [pack(send_sel, spread_sel, tile) for tile in tiles]
-    rows0, moved0 = row_exchange(*packs[0], ny, 0)
-    top0 = unpack_rows(place, rows0)
-    tile0 = unpack_moved(insert, hit, moved0, tiles[0])
-
-    def more(top0, tile0):
-        whole = jnp.concatenate(tiles, axis=1)
-
-        def body(state):
-            r, top, tile = state
-            send_sel, place, spread_sel, insert, hit = plan(r)
-            rows, moved = row_exchange(*pack(send_sel, spread_sel, whole), ny, 1)
-            return r + 1, top + unpack_rows(place, rows), unpack_moved(insert, hit, moved, tile)
-
-        start = jnp.concatenate([top0, jnp.zeros_like(top0)], axis=1), jnp.concatenate([tile0, tiles[1]], axis=1)
-        _, top, tile = lax.while_loop(lambda s: s[0] < rounds, body, (jnp.int32(1),) + start)
-        return top[:, :NB], top[:, NB:], tile[:, :NB], tile[:, NB:]
-
-    def none(top0, tile0):
-        return top0, jnp.zeros_like(top0), tile0, tiles[1]
-
-    top0, extra, tile0, tile1 = lax.cond(rounds > 1, more, none, top0, tile0)
-
-    panel_top = jnp.where(pcol == 0, top0[NB:], top0[:NB])
-    quarter = NB // CORES
-    part = lax.dynamic_slice_in_dim(panel_top, core * quarter, quarter, 0)
-    src_a = jnp.concatenate([part, tile0[:quarter]], axis=0).reshape(nz, NX, PA, NB)
-    src_b = tile0[quarter:].reshape(NX, nz, PB, NB)
-    buf_a, buf_b, other, rows1, moved1 = panel_spread(src_a, src_b, *packs[1], ny, nz, 2)
-
-    top1 = unpack_rows(place, rows1) + extra
-    tile1 = unpack_moved(insert, hit, moved1, tile1)
-    flat_a = buf_a.reshape(2, NB, NB)
-    flat_b = buf_b.reshape(2, 2 * NB - quarter, NB)
-    other = other.reshape(2, quarter, NB)
-    raw = [jnp.concatenate([flat_a[k, quarter:], flat_b[k]], axis=0) for k in (0, 1)]
-    first = jnp.where(core == 0, flat_a[:, :quarter], other)
-    second = jnp.where(core == 0, other, flat_a[:, :quarter])
-    tops = jnp.concatenate([first, second], axis=1)
-
-    l0, l1, u0, u1 = lower_inverse[0], lower_inverse[1], upper_inverse[0], upper_inverse[1]
-    factor0 = bdot(raw[0], u0)
-    corner = bdot(tops[0], u0)
-    upper_panel = bdot(l0, tops[1])
-    panel1 = (raw[1].astype(jnp.float32) - dot(factor0, upper_panel)).astype(jnp.bfloat16)
-    factor1 = bdot(panel1, u1)
-    out = []
-    for d, (top, tile) in enumerate(((top0, tile0), (top1, tile1))):
-        up0 = bdot(l0, top[:NB])
-        low = (top[NB:].astype(jnp.float32) - dot(corner, up0)).astype(jnp.bfloat16)
-        up1 = bdot(l1, low)
-        new = (tile.astype(jnp.float32) - dot(factor0, up0)).astype(jnp.bfloat16)
-        new = (new.astype(jnp.float32) - dot(factor1, up1)).astype(jnp.bfloat16)
-        row0, row1 = up0, up1
-        if d == 0:
-            new = jnp.where(pcol == 0, factor0, jnp.where(pcol == 1, factor1, new))
-            row0 = jnp.where(pcol == 0, top[:NB], up0)
-            row1 = jnp.where(pcol == 0, corner, jnp.where(pcol == 1, low, up1))
-        head = jnp.where(prow == 0, row0, jnp.where(prow == 1, row1, new[:NB]))
-        out.append(jnp.concatenate([head, new[NB:]], axis=0).reshape(2, NB, NB))
-    return jnp.stack(out, axis=2).reshape(matrix.shape)
+        rows, moved = row_exchange(
+            bdot(pick, tile).reshape(2, CAP // 2, 2 * NB),
+            bdot(spread_sel, tile[:NB]).reshape(nprow, DCAP, 2 * NB), ny, 1)
+        place = one_hot(jnp.where(t_in, t_slot, -1), nprow * CAP)
+        top = top + bdot(place, rows.reshape(nprow * CAP, 2 * NB))
+        new = bdot(insert, moved.reshape(MOVED, 2 * NB))
+        return r + 1, top, jnp.where(jnp.any(insert > 0, axis=1)[:, None], new, now)
+
+    _, top, now = lax.while_loop(
+        lambda s: s[0] < rounds, body, (jnp.int32(0), jnp.zeros_like(tile), tile))
+    return top, now
+
+
+def per_device(matrix, pivots, lower_inverse, upper_inverse):
+    nprow, npcol = lax.axis_size("prow"), lax.axis_size("pcol")
+    ny, nz = nprow // CORES, npcol // NX
+    n = 2 * NB
+    tile = matrix.reshape(n, n)
+    *packed, slot, into, rounds = index_and_pack(pivots, tile, nprow)
+
+    def finish(tile, packed, slot, into, known, cids):
+        sents = [v.reshape(2, CAP // 2, NB) for v in packed[:2]]
+        spreads = [v.reshape(nprow, DCAP, NB) for v in packed[2:]]
+        piece, rows0, moved0 = first_exchange(tile, sents[0], spreads[0], ny, nz, cids[0])
+        rows0, moved0 = rows0.reshape(nprow * CAP, NB), moved0.reshape(MOVED, NB)
+        if known is not None:
+            rows0, moved0 = known[0], jnp.zeros_like(moved0)
+        small = panel_tops(rows0, moved0, slot, nz).reshape(NX, nz, PB, NB)
+        raw, extra, other, rows1, moved1 = second_exchange(piece, small, sents[1], spreads[1], ny, nz, cids[1])
+        rows1, moved1 = rows1.reshape(nprow * CAP, NB), moved1.reshape(MOVED, NB)
+        if known is not None:
+            rows1, moved1 = known[1], jnp.zeros_like(moved1)
+        return update(
+            raw.reshape(2, n, NB), extra.reshape(2, NX, nz * PB, NB), other.reshape(2, NX, nz * PB // 2, NB),
+            rows0, rows1, moved0, moved1, slot, into, tile, lower_inverse, upper_inverse)
+
+    def one_round(tile):
+        return finish(tile, packed, slot, into, None, (0, 2))
+
+    def many_rounds(tile):
+        top, now = collect_rounds(tile, pivots, nprow, ny)
+        top = jnp.pad(top, ((0, nprow * CAP - n), (0, 0)))
+        empty = [jnp.zeros_like(v) for v in packed]
+        order = jnp.arange(n, dtype=jnp.int32)[:, None]
+        return finish(now, empty, order, jnp.full_like(into, -1), (top[:, :NB], top[:, NB:]), (3, 4))
+
+    out = lax.cond(rounds[0, 0] > 1, many_rounds, one_round, tile)
+    return out.reshape(matrix.shape)
 
 
 def solution(mesh):

time: 174 us -> 121 us (0.70); the launches traced: 172 us -> 121 us
  matrix products: 35.2 us -> 0 us
  Pallas kernels: 90.4 us -> 114 us
  other arithmetic: 17.7 us -> 0 us
  local copies, waits for them, and re-layouts: 24.2 us -> 6.65 us
  between operations: 4.53 us -> 0.69 us
    dot_general x21 -> x0, matrix products: 35.2 us -> none  [dot(): return jnp.dot(a, b, preferred_element_type=jnp.float32)]
    pallas_call x2 -> x5, Pallas kernels: 90.4 us -> 114 us  [the longest x1 45.9 us: second_exchange(): pl.pallas_call(lambda *refs: second_kernel(ny, nz, len(sems), *refs), out...]
    slice x6 -> x0, local copies, waits for them, and re-layouts: 10.8 us -> none  [the longest x1 6.53 us: per_device(): tiles = [matrix[:, 0, :, d, 0, :].reshape(2 * NB, NB) for d in (0, 1)]]
    reshape x1 -> x0, other arithmetic: 5.63 us -> none  [per_device(): return jnp.stack(out, axis=2).reshape(matrix.shape)]
    select_n x11 -> x0, other arithmetic: 5.09 us -> none  [the longest x2 1.42 us: per_device(): head = jnp.where(prow == 0, row0, jnp.where(prow == 1, row1, new[:NB]))]
    another operation x5 -> x0, local copies, waits for them, and re-layouts: 4.6 us -> none  [the longest x2 3.5 us: per_device(): return jnp.stack(out, axis=2).reshape(matrix.shape)]
    reshape x0 -> x1, local copies, waits for them, and re-layouts: none -> 4.48 us  [per_device(): return out.reshape(matrix.shape)]
    unnamed x52 -> x5, local copies, waits for them, and re-layouts: 6.43 us -> 2.17 us
where the time goes in v2:
time: 121 us
  Pallas kernels  114 us (94%)
  local copies, waits for them, and re-layouts  6.65 us (5%)
    pallas_call x1, Pallas kernels, second_exchange(): pl.pallas_call(lambda *refs: second_kernel(ny, nz, len(sems), *refs), out...  45.9 us
    pallas_call x1, Pallas kernels, first_exchange(): pl.pallas_call(lambda *refs: first_kernel(ny, nz, len(sems), *refs), out_...  35.7 us
    pallas_call x1, Pallas kernels, update(): pl.pallas_call(update_kernel, out_shape=jax.ShapeDtypeStruct((n, n), bf16...  17.9 us
    pallas_call x1, Pallas kernels, index_and_pack(): pl.pallas_call(lambda *refs: index_kernel(nprow, *refs), out_shape=(jax.S...  11.1 us
    reshape x1, local copies, waits for them, and re-layouts, per_device(): return out.reshape(matrix.shape)  4.48 us
    pallas_call x1, Pallas kernels, panel_tops(): pl.pallas_call(panel_tops_kernel, out_shape=jax.ShapeDtypeStruct((NX, nz...  3.01 us

profile of v2, /device:TPU:1, one launch (start us, length us, event | category | flops | bytes accessed | tf_op | source)
XLA Modules:
  0.0 121.0 jit_solution(5058853703554109427)
XLA Ops:
  0.0 0.0 copy-start.2
  0.0 2.2 %copy.9 = bf16[128,8,2,512]{3,1,2,0:T(8,128)(2,1)S(1)} copy(bf16[128,8,2,512]{3,2,1,0:T(2,128)(2,1)} %bitcast.58) | data formatting | bytes 4194304
  2.2 0.0 copy-start.1
  2.2 0.0 copy-done.2
  2.2 11.1 %index_and_pack.1 = (bf16[96,512]{1,0:T(8,128)(2,1)S(1)}, bf16[96,512]{1,0:T(8,128)(2,1)S(1)}, bf16[896,512]{1,0:T(8,128)(2,1)}, bf16[896,512]{1,0:T(8,128)(2,1)...) custom-call(s32[2,512]{1,0:T(2,128)S(1)} %copy-done.2, bf16[1024,1024]{1,0:T(8,128)(2,1)S(1)} %bitcast.50), custom_call_target="tpu_custom_call" | custom-call | tf_op jit(solution)/shard_map/index_and_pack/pallas_call | solution.py:609
  14.0 0.0 copy-done.1
  14.0 102.5 %conditional.1 = (bf16[1024,1024]{1,0:T(8,128)(2,1)}) conditional(s32[]{:T(128)} %bitcast.27, (bf16[96,512]{1,0:T(8,128)(2,1)S(1)}, bf16[896,512]{1,0:T(8,128)(2,1)}, bf16[1024,1024]{1,0:T(8,128)(2,1)S(1)}, s32[1024,1]{1,0:T(8,128)}, bf16[96,512]{1,0:T(8,128)(2,1)S(1)}, /*index=5*/bf16[896,512]{1,0:T(8,128)(2,1)}, s32[1,128]{1,0:T(1,128)S(1)}, ...), branch_computations={%region_0.0_spmd, %region_1.25_spmd} | conditional | flops 4629360128 | bytes 50895452 | solution.py:868
  14.0 35.7 %first_exchange.2 = (bf16[2,32,512]{2,1,0:T(8,128)(2,1)}, bf16[16,2,48,512]{3,2,1,0:T(8,128)(2,1)}, bf16[2,56,512]{2,1,0:T(8,128)(2,1)}) custom-call(bf16[1024,1024]{1,0:T(8,128)(2,1)S(1)} %get-tuple-element.302.refs_0_.tile, bf16[2,48,512]{2,1,0:T(8,128)(2,1)S(1)} %bitcast.83, bf16[16,56,512]{2,1,0:T(8,128)(2,1)} %bitcast.67), custom_call_target="tpu_custom_call" | custom-call | tf_op jit(solution)/shard_map/cond/branch_0_fun/first_exchange/pallas_call | solution.py:336
  49.8 3.0 %panel_tops.2 = bf16[4,128,512]{2,1,0:T(8,128)(2,1)} custom-call(bf16[1536,512]{1,0:T(8,128)(2,1)} %bitcast.55, bf16[112,512]{1,0:T(8,128)(2,1)} %bitcast.74, s32[1024,1]{1,0:T(8,128)} %get-tuple-element.308.slot), custom_call_target="tpu_custom_call" | custom-call | tf_op jit(solution)/shard_map/cond/branch_0_fun/panel_tops/pallas_call | solution.py:643
  52.8 45.9 %second_exchange.2 = (bf16[2,8,4,32,512]{4,3,2,1,0:T(8,128)(2,1)}, bf16[2,4,8,16,512]{4,3,2,1,0:T(8,128)(2,1)}, bf16[2,4,4,16,512]{4,3,2,1,0:T(8,128)(2,1)}, bf1...) custom-call(bf16[2,32,512]{2,1,0:T(8,128)(2,1)} %get-tuple-element.305.refs_0_, bf16[4,8,16,512]{3,2,1,0:T(8,128)(2,1)} %bitcast.60, ...), custom_call_target="tpu_custom_call" | custom-call | tf_op jit(solution)/shard_map/cond/branch_0_fun/second_exchange/pallas_call | solution.py:462
  98.6 17.9 %update.2 = bf16[1024,1024]{1,0:T(8,128)(2,1)} custom-call(bf16[2,1024,512]{2,1,0:T(8,128)(2,1)} %bitcast.62, bf16[2,4,128,512]{3,2,1,0:T(8,128)(2,1)} %bitcast.65, bf16[2,4,64,512]{3,2,1,0:T(8,128)(2,1)} %bitcast.69, bf16[1536,512]{1,0:T(8,128)(2,1)} %bitcast.56, bf16[1536,512]{1,0:T(8,128)(2,1)} %bitcast.63, bf16[112,512]{1,0:T(8,128)(2,1)} %bitcast.75, ...), custom_call_target="tpu_custom_call" | custom-call | tf_op jit(solution)/shard_map/cond/branch_0_fun/update/pallas_call | solution.py:731
  116.5 4.5 %reshape.404 = bf16[2,1,512,2,1,512]{5,3,2,0,4,1:T(2,128)(2,1)} reshape(bf16[1024,1024]{1,0:T(8,128)(2,1)} %get-tuple-element.369) | data formatting | bytes 4194304 | tf_op jit(solution)/shard_map/reshape | solution.py:869
Async XLA Ops:
  0.0 2.2 %copy-start.2 = (s32[2,512]{1,0:T(2,128)S(1)}, s32[2,512]{1,0:T(2,128)}, u32[]{:S(2)}) copy-start(s32[2,512]{1,0:T(2,128)} %refs_0_.1) | copy-start | bytes 12292
  2.2 11.8 %copy-start.1 = (bf16[2,512,512]{2,1,0:T(8,128)(2,1)S(1)}, bf16[2,512,512]{2,1,0:T(8,128)(2,1)}, u32[]{:S(2)}) copy-start(bf16[2,512,512]{2,1,0:T(8,128)(2,1)} %param.10) | copy-start | bytes 3145732

commit v3 on v2

--- a/solution.py
+++ b/solution.py
@@ -12,9 +12,11 @@
 DCAP = 56
 MOVED = CORES * DCAP
 HALF = NB // CORES
+LANES = NB // NX
 PA = 32
-PB = 16
+PB = 48
 MESH = pl.DeviceIdType.MESH
+T_Y, T_A0, T_A1, T_AD, T_BZ, T_BX, T_BXD = 4.5, 0.0, 2.5, 5.8, 4.5, 13.0, 4.0
 ANY = pl.BlockSpec(memory_space=pl.ANY)
 
 
@@ -311,21 +313,61 @@
                 self.copy(k).wait_send()
 
 
+class Direct:
+    def __init__(self, n, pos, goto, item, send, recv):
+        self.n, self.pos, self.goto, self.item, self.send, self.recv = n, pos, goto, item, send, recv
+
+    def copy(self, k, half):
+        to = lax.rem(self.pos + k, self.n)
+        return pltpu.make_async_remote_copy(
+            src_ref=self.item(self.pos, half), dst_ref=self.item(self.pos, half),
+            send_sem=self.send.at[k, half], recv_sem=self.recv.at[k, half],
+            device_id=self.goto(to), device_id_type=MESH)
+
+    def start(self):
+        for half in (0, 1):
+            self.start_half(half)
+
+    def start_half(self, half):
+        for k in sorted(range(1, self.n), key=lambda k: -min(k, self.n - k)):
+            self.copy(k, half).start()
+
+    def wait(self, half):
+        for k in range(1, self.n):
+            ref = self.item(lax.rem(self.pos + self.n - k, self.n), half)
+            pltpu.make_async_copy(ref, ref, self.recv.at[k, half]).wait()
+
+    def drain(self):
+        for half in (0, 1):
+            for k in range(1, self.n):
+                self.copy(k, half).wait_send()
+
+
 def first_kernel(ny, nz, nexch, *refs):
-    tile, sent, spread, piece, rows, moved = refs[:6]
+    tile, sent, spread, line, rows, moved = refs[:6]
     ex = RowExchange(ny, sent, spread, rows, moved, refs[6 : 6 + nexch])
-    ss, sr = refs[6 + nexch :]
+    ss, sr, xs, xr = refs[6 + nexch :]
     pcol = lax.axis_index("pcol")
     n = nz * NX
+    z, x = lax.div(pcol, NX), lax.rem(pcol, NX)
     scatter = Scatter(
         pcol, n,
         lambda to: tile.at[pl.ds(pl.multiple_of(to * PA, PA), PA), pl.ds(0, NB)],
-        lambda panel, to: piece.at[panel], ss, sr)
-    meet_with_roots(ex.barrier_peers(), pcol, n)
-    run_events(ex.events(3.8) + [(0.0, scatter.start)])
+        lambda panel, to: line.at[panel, lax.rem(to, NX)], ss, sr)
+    gather = Direct(NX, x, lambda i: {"pcol": z * NX + i}, lambda i, h: line.at[h, i], xs, xr)
+    near = ex.barrier_peers() + [{"pcol": z * NX + lax.rem(x + d, NX)} for d in range(1, NX)]
+    meet_with_roots(near, pcol, n)
+
+    def pass_on():
+        for panel in (0, 1):
+            scatter.landed(panel)
+            gather.start_half(panel)
+
+    run_events(ex.events(3.8) + [(-0.5, scatter.start), (13.0, pass_on)])
     ex.finish()
     for panel in (0, 1):
-        scatter.landed(panel)
+        gather.wait(panel)
+    gather.drain()
     scatter.drain()
 
 
@@ -336,51 +378,22 @@
     return pl.pallas_call(
         lambda *refs: first_kernel(ny, nz, len(sems), *refs),
         out_shape=(
-            jax.ShapeDtypeStruct((2, PA, NB), jnp.bfloat16),
+            jax.ShapeDtypeStruct((2, NX, PA, NB), jnp.bfloat16),
             jax.ShapeDtypeStruct((ny * CORES, 2, CAP // 2, width), jnp.bfloat16),
             jax.ShapeDtypeStruct((CORES, DCAP, width), jnp.bfloat16),
         ),
         in_specs=[ANY] * 3,
         out_specs=(ANY,) * 3,
-        scratch_shapes=sems + [dma((nz * NX,)), dma((2,))],
+        scratch_shapes=sems + [dma((nz * NX,)), dma((2,)), dma((NX, 2)), dma((NX, 2))],
         compiler_params=pltpu.CompilerParams(collective_id=cid, has_side_effects=True),
         name="first_exchange",
     )(tile, sent, spread)
 
 
-class Direct:
-    def __init__(self, n, pos, goto, item, fresh, send, recv):
-        self.n, self.pos, self.goto, self.item, self.fresh, self.send, self.recv = n, pos, goto, item, fresh, send, recv
-
-    def copy(self, k, half):
-        to = lax.rem(self.pos + k, self.n)
-        return pltpu.make_async_remote_copy(
-            src_ref=self.fresh(half), dst_ref=self.item(self.pos, half),
-            send_sem=self.send.at[k, half], recv_sem=self.recv.at[k, half],
-            device_id=self.goto(to), device_id_type=MESH)
-
-    def start(self):
-        for half in (0, 1):
-            for k in range(1, self.n):
-                self.copy(k, half).start()
-            pltpu.make_async_copy(
-                self.fresh(half), self.item(self.pos, half), self.recv.at[0, half]).start()
-
-    def wait(self, half):
-        for k in range(self.n):
-            ref = self.item(lax.rem(self.pos + self.n - k, self.n), half)
-            pltpu.make_async_copy(ref, ref, self.recv.at[k, half]).wait()
-
-    def drain(self):
-        for half in (0, 1):
-            for k in range(1, self.n):
-                self.copy(k, half).wait_send()
-
-
 def second_kernel(ny, nz, nexch, *refs):
-    piece, small, sent, spread, raw, extra, other, rows, moved = refs[:9]
+    line, small, sent, spread, raw, extra, other, rows, moved = refs[:9]
     ex = RowExchange(ny, sent, spread, rows, moved, refs[9 : 9 + nexch])
-    (axs, axr, azs, azr, bzs, bzr, bxs, bxr, ss, sr, ts, tr, to_s, to_r) = refs[9 + nexch :]
+    (azs, azr, bzs, bzr, bxs, bxr, ss, sr, ts, tr, to_s, to_r, own) = refs[9 + nexch :]
     pcol = lax.axis_index("pcol")
     n = nz * NX
     z, x = lax.div(pcol, NX), lax.rem(pcol, NX)
@@ -392,16 +405,14 @@
         return {"pcol": i * NX + x}
 
     near = ex.barrier_peers()
-    near += [to_x(lax.rem(x + d, NX)) for d in range(1, NX)]
-    near += [to_z(lax.rem(z + d, nz)) for d in (1, nz - 1)]
+    near += [to_x(lax.rem(x + d, NX)) for d in (1, NX - 1)]
+    near += [to_z(lax.rem(z + d, nz)) for d in range(1, nz)]
     meet_with_roots(near, pcol, n)
 
-    tops = nz // 2
-
-    def across(index, way, hop, half, sems=None):
+    def across(index, way, hop, half):
         s, r = (ts.at[way, hop - 1, half], tr.at[way, hop - 1, half]) if hop else (to_s.at[half], to_r.at[half])
         return pltpu.make_async_remote_copy(
-            src_ref=extra.at[half, index, pl.ds(0, tops)], dst_ref=other.at[half, index],
+            src_ref=extra.at[half, index, pl.ds(0, HALF)], dst_ref=other.at[half, index],
             send_sem=s, recv_sem=r, device_id=ex.partner, device_id_type=MESH)
 
     crossing = []
@@ -411,71 +422,76 @@
         copy.start()
         crossing.append(copy)
 
+    def band(i):
+        return pl.ds(pl.multiple_of(i * PB, PB), PB)
+
     scatter = Scatter(
         pcol, n,
-        lambda to: small.at[lax.rem(to, NX), lax.div(to, NX)],
-        lambda panel, to: extra.at[panel, lax.rem(to, NX), lax.div(to, NX)], ss, sr)
-    ax = Direct(NX, x, to_x, lambda i, h: raw.at[h, z, i], lambda h: piece.at[h], axs, axr)
-    az = Ring(nz, z, to_z, lambda i, h: raw.at[h, i], azs, azr)
-    bz = Ring(nz, z, to_z, lambda i, h: extra.at[h, x, i], bzs, bzr)
+        lambda to: small.at[lax.rem(to, NX), band(lax.div(to, NX))],
+        lambda panel, to: extra.at[panel, lax.rem(to, NX), band(lax.div(to, NX))], ss, sr)
+    az = Ring(nz, z, to_z, lambda i, h: raw.at[h, i], azs, azr, fresh=lambda h: line.at[h])
+    bz = Direct(nz, z, to_z, lambda i, h: extra.at[h, x, band(i)], bzs, bzr)
     bx = Ring(NX, x, to_x, lambda i, h: extra.at[h, i], bxs, bxr, arrived=cross)
-
-    def begin_az(half):
-        ax.wait(half)
-        az.start(half)
-
-    def begin_bz(half):
-        scatter.landed(half)
-        bz.start(half)
+    keep = [pltpu.make_async_copy(line.at[h], raw.at[h, z], own.at[h]) for h in (0, 1)]
+
+    def begin_az():
+        for half in (0, 1):
+            az.start(half)
+        for copy in keep:
+            copy.start()
+
+    def begin_bz():
+        for half in (0, 1):
+            scatter.landed(half)
+            bz.start_half(half)
 
     def begin_bx(half):
-        bz.complete(half)
+        bz.wait(half)
         bx.start(half)
         cross(x, None, 0, 0, half)
 
-    events = [(-0.6, scatter.start), (-0.5, ax.start)]
-    events += ex.events(4.5)
-    events += [(3.5 + h * 0.3, lambda h=h: begin_az(h)) for h in (0, 1)]
-    events += az.events([3.5, 5.5], 5.0)
-    events += [(5.0 + h * 0.1, lambda h=h: begin_bz(h)) for h in (0, 1)]
-    events += bz.events([5.2, 5.4], 3.0)
-    events += [(17.6 + h * 0.1, lambda h=h: begin_bx(h)) for h in (0, 1)]
-    events += bx.events([18.0, 19.5], 3.5)
+    events = [(-2.0, scatter.start), (-0.9, begin_az)]
+    events += ex.events(T_Y)
+    events += az.events([T_A0, T_A1], T_AD)
+    events += [(T_BZ, begin_bz)]
+    events += [(T_BX + h * 0.4, lambda h=h: begin_bx(h)) for h in (0, 1)]
+    events += bx.events([T_BX + 0.2, T_BX + 1.2], T_BXD)
     run_events(events)
     ex.finish()
-    for ring in (az, bz, bx):
+    for ring in (az, bx):
         for half in (0, 1):
             ring.complete(half)
         ring.drain()
-    ax.drain()
+    bz.drain()
     scatter.drain()
     for copy in crossing:
         copy.wait()
-
-
-def second_exchange(piece, small, sent, spread, ny, nz, cid):
+    for copy in keep:
+        copy.wait()
+
+
+def second_exchange(line, small, sent, spread, ny, nz, cid):
     width = sent.shape[-1]
     dma = pltpu.SemaphoreType.DMA
     sems = exchange_sems(ny)
-    zring, xring = dma((2, nz // 2, 2)), dma((2, NX // 2, 2))
-    direct = dma((NX, 2))
+    zring, xring, zdirect = dma((2, nz // 2, 2)), dma((2, NX // 2, 2)), dma((nz, 2))
     return pl.pallas_call(
         lambda *refs: second_kernel(ny, nz, len(sems), *refs),
         out_shape=(
             jax.ShapeDtypeStruct((2, nz, NX, PA, NB), jnp.bfloat16),
-            jax.ShapeDtypeStruct((2, NX, nz, PB, NB), jnp.bfloat16),
-            jax.ShapeDtypeStruct((2, NX, nz // 2, PB, NB), jnp.bfloat16),
+            jax.ShapeDtypeStruct((2, NX, nz * PB, LANES), jnp.bfloat16),
+            jax.ShapeDtypeStruct((2, NX, HALF, LANES), jnp.bfloat16),
             jax.ShapeDtypeStruct((ny * CORES, 2, CAP // 2, width), jnp.bfloat16),
             jax.ShapeDtypeStruct((CORES, DCAP, width), jnp.bfloat16),
         ),
         in_specs=[ANY] * 4,
         out_specs=(ANY,) * 5,
         scratch_shapes=sems
-        + [direct, direct, zring, zring, zring, zring, xring, xring]
-        + [dma((nz * NX,)), dma((2,)), xring, xring, dma((2,)), dma((2,))],
+        + [zring, zring, zdirect, zdirect, xring, xring]
+        + [dma((nz * NX,)), dma((2,)), xring, xring, dma((2,)), dma((2,)), dma((2,))],
         compiler_params=pltpu.CompilerParams(collective_id=cid, has_side_effects=True),
         name="second_exchange",
-    )(piece, small, sent, spread)
+    )(line, small, sent, spread)
 
 
 def dot(a, b):
@@ -547,46 +563,40 @@
         return (lax.shift_right_logical(v, 13) * NB + (v & (NB - 1))).astype(jnp.float32)
 
     n = 2 * NB
-    e0, e1 = ids((n, n), 0), ids((n, n), 1)
-
-    def rank(group_c):
-        group_r = to_row(group_c)
-        same = group_c == group_r
-        rank_c = along(jnp.where(same & (e1 < e0), 1.0, 0.0))
-        rank_r = down(jnp.where(same & (e0 < e1), 1.0, 0.0))
-        return group_r, rank_c, rank_r
-
     t_c = jnp.concatenate([cols[0], src1], axis=0)
-    t_group = owner(t_c)
-    t_group_r, t_rank_c, t_rank_r = rank(t_group)
-    slot_c = jnp.where(t_rank_c < CAP, t_group * CAP + t_rank_c, -1.0)
-    slot_r = jnp.where(t_rank_r < CAP, t_group_r * CAP + t_rank_r, -1.0)
-    slot_out[...] = slot_c.astype(jnp.int32)
-    mine = ids((CAP, 1), 0) + prow_f * CAP
-    pick = along(jnp.where(slot_r == mine, local(to_row(t_c)) + 1.0, 0.0)) - 1.0
-    sent = bdot(hot(pick == ids((CAP, n), 1)), tile[...])
-    sent0[...] = sent[:, :NB]
-    sent1[...] = sent[:, NB:]
-
     d_dst = jnp.concatenate([cols[0], cols[1]], axis=0)
     d_src = jnp.concatenate([receive[0], from1], axis=0)
     fresh = jnp.concatenate([again, jnp.zeros_like(again)], axis=0)
     valid = (d_dst >= 2.0 * NB) & (fresh < 0.5)
-    group = jnp.where(valid, owner(d_dst) * CORES + jnp.where(d_src >= NB, 1.0, 0.0), -1.0)
-    group_r, rank_c, rank_r = rank(group)
-    key_c = jnp.where(valid & (rank_c < DCAP), group * DCAP + rank_c, -1.0)
+    t_group = owner(t_c)
+    group = jnp.where(valid, owner(d_dst) * CORES + jnp.where(d_src >= NB, 1.0, 0.0), -1000.0)
+    lanes = ids((n, 128), 1)
+    members = jnp.where((lanes == t_group) | (lanes == group + nprow), 1.0, 0.0)
+    before = dot(hot(ids((n, n), 1) < ids((n, n), 0)), members.astype(jnp.bfloat16)) * members
+    is_t = lanes < nprow
+    t_rank = along(jnp.where(is_t, before, 0.0))
+    d_rank = along(jnp.where(is_t, 0.0, before))
+    slot_c = jnp.where(t_rank < CAP, t_group * CAP + t_rank, -1.0)
+    key_c = jnp.where(valid & (d_rank < DCAP), group * DCAP + d_rank, -1.0)
+    slot_out[...] = slot_c.astype(jnp.int32)
+    packed = jnp.where(lanes == 0, slot_c, jnp.where(lanes == 1, local(t_c), jnp.where(lanes == 2, key_c, d_src)))
+    packed = packed.T
+    slot_r, local_r, key_r, src_r = (packed[k : k + 1, :] for k in range(4))
+    mine = ids((CAP, 1), 0) + prow_f * CAP
+    pick = along(jnp.where(slot_r == mine, local_r + 1.0, 0.0)) - 1.0
+    sent = bdot(hot(pick == ids((CAP, n), 1)), tile[...])
+    sent0[...] = sent[:, :NB]
+    sent1[...] = sent[:, NB:]
     lane = ids((1, 128), 1)
     wanted = jnp.where(lane < MOVED, lane + prow_f * MOVED, -2.0)
     into = down(jnp.where(key_c == wanted, local(d_dst) + 1.0, 0.0)) - 1.0
     into_out[...] = into.astype(jnp.int32)
-    most_t = jnp.max(t_rank_c) * (1.0 / CAP)
-    most_d = jnp.max(jnp.where(valid, rank_c, 0.0)) * (1.0 / DCAP)
+    most_t = jnp.max(t_rank) * (1.0 / CAP)
+    most_d = jnp.max(jnp.where(valid, d_rank, 0.0)) * (1.0 / DCAP)
     rounds_out[0, 0] = jnp.where(jnp.maximum(most_t, most_d) > 1.0 - 0.25 / CAP, 2, 1).astype(jnp.int32)
 
     @pl.when(prow < CORES)
     def _():
-        key_r = jnp.where((group_r > -0.5) & (rank_r < DCAP), group_r * DCAP + rank_r, -1.0)
-        src_r = to_row(d_src)
         s = ids((MOVED, 1), 0)
 
         def one_chip(q, _):
@@ -628,21 +638,19 @@
     total = rows.shape[0]
     place = jnp.where(keys == lax.broadcasted_iota(jnp.int32, (HALF, total), 1), 1.0, 0.0).astype(jnp.bfloat16)
     part = bdot(place, rows[...])
-    step = HALF // NX
+    last = small.shape[1] - HALF - MOVED
     for x in range(NX):
-        small[x, pl.ds(0, step), :] = part[x * step : (x + 1) * step]
-    small[0, pl.ds(step, step), :] = moved[pl.ds(0, step), :]
-    small[1, pl.ds(step, MOVED - step), :] = moved[pl.ds(step, MOVED - step), :]
-    for x, start in ((1, MOVED), (2, step), (3, step)):
-        size = 2 * step - start if x > 1 else 2 * step - MOVED
-        small[x, pl.ds(2 * step - size, size), :] = jnp.zeros((size, NB), jnp.bfloat16)
+        lanes = slice(x * LANES, (x + 1) * LANES)
+        small[x, pl.ds(0, HALF), :] = part[:, lanes]
+        small[x, pl.ds(HALF, MOVED), :] = moved[:, lanes]
+        small[x, pl.ds(HALF + MOVED, last), :] = jnp.zeros((last, LANES), jnp.bfloat16)
 
 
 def panel_tops(rows, moved, slot, nz):
     vmem = pl.BlockSpec(memory_space=pltpu.VMEM)
     return pl.pallas_call(
         panel_tops_kernel,
-        out_shape=jax.ShapeDtypeStruct((NX, nz * PB, NB), jnp.bfloat16),
+        out_shape=jax.ShapeDtypeStruct((NX, nz * PB, LANES), jnp.bfloat16),
         in_specs=[vmem] * 3,
         out_specs=vmem,
         name="panel_tops",
@@ -671,16 +679,15 @@
     lax.fori_loop(0, 4, place_rows, 0)
     l0, l1, u0, u1 = low_inv[0], low_inv[1], up_inv[0], up_inv[1]
     panel_tops = []
-    half = HALF // NX
     for k in (0, 1):
-        own = jnp.concatenate([extra[k, x, :half, :] for x in range(NX)], axis=0)
-        far = jnp.concatenate([other[k, x] for x in range(NX)], axis=0)
+        own = jnp.concatenate([extra[k, x, :HALF, :] for x in range(NX)], axis=1)
+        far = jnp.concatenate([other[k, x] for x in range(NX)], axis=1)
         panel_tops.append(jnp.concatenate(
             [jnp.where(core == 0, own, far), jnp.where(core == 0, far, own)], axis=0))
     corner = bdot(panel_tops[0], u0)
     upper = bdot(l0, panel_tops[1])
     moved_panel = [
-        jnp.concatenate([extra[k, 0, half:, :], extra[k, 1, half : half + MOVED - half, :]], axis=0) for k in (0, 1)
+        jnp.concatenate([extra[k, x, HALF : HALF + MOVED, :] for x in range(NX)], axis=1) for k in (0, 1)
     ]
     for cols in halves:
         up0[:, cols] = bdot(l0, top[pl.ds(0, NB), cols])
@@ -842,18 +849,17 @@
     def finish(tile, packed, slot, into, known, cids):
         sents = [v.reshape(2, CAP // 2, NB) for v in packed[:2]]
         spreads = [v.reshape(nprow, DCAP, NB) for v in packed[2:]]
-        piece, rows0, moved0 = first_exchange(tile, sents[0], spreads[0], ny, nz, cids[0])
+        line, rows0, moved0 = first_exchange(tile, sents[0], spreads[0], ny, nz, cids[0])
         rows0, moved0 = rows0.reshape(nprow * CAP, NB), moved0.reshape(MOVED, NB)
         if known is not None:
             rows0, moved0 = known[0], jnp.zeros_like(moved0)
-        small = panel_tops(rows0, moved0, slot, nz).reshape(NX, nz, PB, NB)
-        raw, extra, other, rows1, moved1 = second_exchange(piece, small, sents[1], spreads[1], ny, nz, cids[1])
+        small = panel_tops(rows0, moved0, slot, nz)
+        raw, extra, other, rows1, moved1 = second_exchange(line, small, sents[1], spreads[1], ny, nz, cids[1])
         rows1, moved1 = rows1.reshape(nprow * CAP, NB), moved1.reshape(MOVED, NB)
         if known is not None:
             rows1, moved1 = known[1], jnp.zeros_like(moved1)
         return update(
-            raw.reshape(2, n, NB), extra.reshape(2, NX, nz * PB, NB), other.reshape(2, NX, nz * PB // 2, NB),
-            rows0, rows1, moved0, moved1, slot, into, tile, lower_inverse, upper_inverse)
+            raw.reshape(2, n, NB), extra, other, rows0, rows1, moved0, moved1, slot, into, tile, lower_inverse, upper_inverse)
 
     def one_round(tile):
         return finish(tile, packed, slot, into, None, (0, 2))

time: 121 us -> 110 us (0.909)
  Pallas kernels: 114 us -> 102 us
    pallas_call x1, Pallas kernels: 45.9 us -> 36.1 us  [second_exchange(): pl.pallas_call(lambda *refs: second_kernel(ny, nz, len(sems), *refs), out...]
    pallas_call x1, Pallas kernels: 11.1 us -> 9.27 us  [index_and_pack(): pl.pallas_call(lambda *refs: index_kernel(nprow, *refs), out_shape=(jax.S...]
where the time goes in v3:
time: 110 us
  Pallas kernels  102 us (93%)
  local copies, waits for them, and re-layouts  6.65 us (6%)
    pallas_call x1, Pallas kernels, second_exchange(): pl.pallas_call(lambda *refs: second_kernel(ny, nz, len(sems), *refs), out...  36.1 us
    pallas_call x1, Pallas kernels, first_exchange(): pl.pallas_call(lambda *refs: first_kernel(ny, nz, len(sems), *refs), out_...  35.9 us
    pallas_call x1, Pallas kernels, update(): pl.pallas_call(update_kernel, out_shape=jax.ShapeDtypeStruct((n, n), bf16...  17.9 us
    pallas_call x1, Pallas kernels, index_and_pack(): pl.pallas_call(lambda *refs: index_kernel(nprow, *refs), out_shape=(jax.S...  9.27 us
    reshape x1, local copies, waits for them, and re-layouts, per_device(): return out.reshape(matrix.shape)  4.48 us
    pallas_call x1, Pallas kernels, panel_tops(): pl.pallas_call(panel_tops_kernel, out_shape=jax.ShapeDtypeStruct((NX, nz...  2.96 us

profile of v3, /device:TPU:1, one launch (start us, length us, event | category | flops | bytes accessed | tf_op | source)
XLA Modules:
  0.0 109.5 jit_solution(17533800306961782297)
XLA Ops:
  0.0 0.0 copy-start.2
  0.0 2.2 %copy.9 = bf16[128,8,2,512]{3,1,2,0:T(8,128)(2,1)S(1)} copy(bf16[128,8,2,512]{3,2,1,0:T(2,128)(2,1)} %bitcast.52) | data formatting | bytes 4194304
  2.2 0.0 copy-start.1
  2.2 0.0 copy-done.2
  2.2 9.3 %index_and_pack.1 = (bf16[96,512]{1,0:T(8,128)(2,1)S(1)}, bf16[96,512]{1,0:T(8,128)(2,1)S(1)}, bf16[896,512]{1,0:T(8,128)(2,1)}, bf16[896,512]{1,0:T(8,128)(2,1)...) custom-call(s32[2,512]{1,0:T(2,128)S(1)} %copy-done.2, bf16[1024,1024]{1,0:T(8,128)(2,1)S(1)} %bitcast.44), custom_call_target="tpu_custom_call" | custom-call | tf_op jit(solution)/shard_map/index_and_pack/pallas_call | solution.py:619
  12.1 0.0 copy-done.1
  12.1 92.9 %conditional.1 = (bf16[1024,1024]{1,0:T(8,128)(2,1)}) conditional(s32[]{:T(128)} %bitcast.21, (bf16[96,512]{1,0:T(8,128)(2,1)S(1)}, bf16[896,512]{1,0:T(8,128)(2,1)}, bf16[1024,1024]{1,0:T(8,128)(2,1)S(1)}, s32[1024,1]{1,0:T(8,128)}, bf16[96,512]{1,0:T(8,128)(2,1)S(1)}, /*index=5*/bf16[896,512]{1,0:T(8,128)(2,1)}, s32[1,128]{1,0:T(1,128)S(1)}, ...), branch_computations={%region_0.0_spmd, %region_1.25_spmd} | conditional | flops 4629360128 | bytes 50895452 | solution.py:874
  12.1 35.9 %first_exchange.2 = (bf16[2,4,32,512]{3,2,1,0:T(8,128)(2,1)}, bf16[16,2,48,512]{3,2,1,0:T(8,128)(2,1)}, bf16[2,56,512]{2,1,0:T(8,128)(2,1)}) custom-call(bf16[1024,1024]{1,0:T(8,128)(2,1)S(1)} %get-tuple-element.302.refs_0_.tile, bf16[2,48,512]{2,1,0:T(8,128)(2,1)S(1)} %bitcast.71, bf16[16,56,512]{2,1,0:T(8,128)(2,1)} %bitcast.57), custom_call_target="tpu_custom_call" | custom-call | tf_op jit(solution)/shard_map/cond/branch_0_fun/first_exchange/pallas_call | solution.py:378
  48.1 3.0 %panel_tops.2.refs_1_ = bf16[4,384,128]{2,1,0:T(8,128)(2,1)} custom-call(bf16[1536,512]{1,0:T(8,128)(2,1)} %bitcast.49, bf16[112,512]{1,0:T(8,128)(2,1)} %bitcast.62, s32[1024,1]{1,0:T(8,128)} %get-tuple-element.308.slot), custom_call_target="tpu_custom_call" | custom-call | tf_op jit(solution)/shard_map/cond/branch_0_fun/panel_tops/pallas_call | solution.py:651
  51.0 36.1 %second_exchange.2 = (bf16[2,8,4,32,512]{4,3,2,1,0:T(8,128)(2,1)}, bf16[2,4,384,128]{3,2,1,0:T(8,128)(2,1)}, bf16[2,4,256,128]{3,2,1,0:T(8,128)(2,1)}, bf16[16,2...) custom-call(bf16[2,4,32,512]{3,2,1,0:T(8,128)(2,1)} %get-tuple-element.305.refs_0_, bf16[4,384,128]{2,1,0:T(8,128)(2,1)} %panel_tops.2.refs_1_, ...), custom_call_target="tpu_custom_call" | custom-call | tf_op jit(solution)/shard_map/cond/branch_0_fun/second_exchange/pallas_call | solution.py:478
  87.2 17.9 %update.2 = bf16[1024,1024]{1,0:T(8,128)(2,1)} custom-call(bf16[2,1024,512]{2,1,0:T(8,128)(2,1)} %bitcast.54, bf16[2,4,384,128]{3,2,1,0:T(8,128)(2,1)} %get-tuple-element.312.extra, bf16[2,4,256,128]{3,2,1,0:T(8,128)(2,1)} %get-tuple-element.313.other, bf16[1536,512]{1,0:T(8,128)(2,1)} %bitcast.50, bf16[1536,512]{1,0:T(8,128)(2,1)} %bitcast.55, ...), custom_call_target="tpu_custom_call" | custom-call | tf_op jit(solution)/shard_map/cond/branch_0_fun/update/pallas_call | solution.py:738
  105.0 4.5 %reshape.386 = bf16[2,1,512,2,1,512]{5,3,2,0,4,1:T(2,128)(2,1)} reshape(bf16[1024,1024]{1,0:T(8,128)(2,1)} %get-tuple-element.369) | data formatting | bytes 4194304 | tf_op jit(solution)/shard_map/reshape | solution.py:875
Async XLA Ops:
  0.0 2.2 %copy-start.2 = (s32[2,512]{1,0:T(2,128)S(1)}, s32[2,512]{1,0:T(2,128)}, u32[]{:S(2)}) copy-start(s32[2,512]{1,0:T(2,128)} %refs_0_.1) | copy-start | bytes 12292
  2.2 10.0 %copy-start.1 = (bf16[2,512,512]{2,1,0:T(8,128)(2,1)S(1)}, bf16[2,512,512]{2,1,0:T(8,128)(2,1)}, u32[]{:S(2)}) copy-start(bf16[2,512,512]{2,1,0:T(8,128)(2,1)} %param.10) | copy-start | bytes 3145732

commit v4 on v3

--- a/solution.py
+++ b/solution.py
@@ -16,7 +16,7 @@
 PA = 32
 PB = 48
 MESH = pl.DeviceIdType.MESH
-T_Y, T_A0, T_A1, T_AD, T_BZ, T_BX, T_BXD = 4.5, 0.0, 2.5, 5.8, 4.5, 13.0, 4.0
+T_Y, T_A0, T_A1, T_AD, T_BZ, T_BX, T_BXD, T_TOP = 4.5, 0.0, 2.5, 5.8, 3.5, 11.0, 4.0, 20.5
 ANY = pl.BlockSpec(memory_space=pl.ANY)
 
 
@@ -254,7 +254,7 @@
     )(sent, spread)
 
 
-def meet_with_roots(near, pcol, n):
+def meet_with_roots(near, pcol, n, meanwhile=None):
     barrier = pltpu.get_barrier_semaphore()
 
     def signal(peer):
@@ -272,6 +272,8 @@
 
     for peer in near:
         signal(peer)
+    if meanwhile is not None:
+        meanwhile()
 
     @pl.when(pcol < 2)
     def _():
@@ -391,9 +393,11 @@
 
 
 def second_kernel(ny, nz, nexch, *refs):
-    line, small, sent, spread, raw, extra, other, rows, moved = refs[:9]
-    ex = RowExchange(ny, sent, spread, rows, moved, refs[9 : 9 + nexch])
-    (azs, azr, bzs, bzr, bxs, bxr, ss, sr, ts, tr, to_s, to_r, own) = refs[9 + nexch :]
+    line, rows_first, moved_first, slot_in, sent, spread, raw, extra, other, moved, top = refs[:11]
+    rows, rows0, moved0, slot, made, small, fetch_sem, small_sem = refs[11:19]
+    ex = RowExchange(ny, sent, spread, rows, moved, refs[19 : 19 + nexch])
+    (azs, azr, bzs, bzr, bxs, bxr, ss, sr, ts, tr, to_s, to_r, own) = refs[19 + nexch :]
+    total = rows0.shape[0]
     pcol = lax.axis_index("pcol")
     n = nz * NX
     z, x = lax.div(pcol, NX), lax.rem(pcol, NX)
@@ -407,7 +411,44 @@
     near = ex.barrier_peers()
     near += [to_x(lax.rem(x + d, NX)) for d in (1, NX - 1)]
     near += [to_z(lax.rem(z + d, nz)) for d in range(1, nz)]
-    meet_with_roots(near, pcol, n)
+
+    def place(start, size):
+        keys = slot[pl.ds(pl.multiple_of(start, HALF), size), :]
+        return jnp.where(
+            keys == lax.broadcasted_iota(jnp.int32, (size, total), 1), 1.0, 0.0
+        ).astype(jnp.bfloat16)
+
+    def place_rows(source, cols):
+        def chunk(i, _):
+            here = pl.ds(pl.multiple_of(i * HALF, HALF), HALF)
+            top[here, cols] = bdot(place(i * HALF, HALF), source())
+            return 0
+
+        lax.fori_loop(0, 2 * NB // HALF, chunk, 0)
+
+    def meanwhile():
+        fetches = [
+            pltpu.make_async_copy(src, dst, fetch_sem.at[k])
+            for k, (src, dst) in enumerate(((slot_in, slot), (moved_first, moved0), (rows_first, rows0)))
+        ]
+        for copy in fetches:
+            copy.start()
+        for copy in fetches:
+            copy.wait()
+        first = jnp.where(pcol == 0, NB, 0) + ex.c * HALF
+        part = bdot(place(first, HALF), rows0[...])
+        last = made.shape[1] - HALF - MOVED
+        for k in range(NX):
+            lanes = slice(k * LANES, (k + 1) * LANES)
+            made[k, pl.ds(0, HALF), :] = part[:, lanes]
+            made[k, pl.ds(HALF, MOVED), :] = moved0[:, lanes]
+            made[k, pl.ds(HALF + MOVED, last), :] = jnp.zeros((last, LANES), jnp.bfloat16)
+        place_rows(lambda: rows0[...], pl.ds(0, NB))
+        handover = pltpu.make_async_copy(made, small, small_sem)
+        handover.start()
+        handover.wait()
+
+    meet_with_roots(near, pcol, n, meanwhile)
 
     def across(index, way, hop, half):
         s, r = (ts.at[way, hop - 1, half], tr.at[way, hop - 1, half]) if hop else (to_s.at[half], to_r.at[half])
@@ -456,8 +497,13 @@
     events += [(T_BZ, begin_bz)]
     events += [(T_BX + h * 0.4, lambda h=h: begin_bx(h)) for h in (0, 1)]
     events += bx.events([T_BX + 0.2, T_BX + 1.2], T_BXD)
+
+    def last_rows():
+        ex.finish()
+        place_rows(lambda: rows[...].reshape(total, NB), pl.ds(NB, NB))
+
+    events += [(T_TOP, last_rows)]
     run_events(events)
-    ex.finish()
     for ring in (az, bx):
         for half in (0, 1):
             ring.complete(half)
@@ -470,7 +516,7 @@
         copy.wait()
 
 
-def second_exchange(line, small, sent, spread, ny, nz, cid):
+def second_exchange(line, rows0, moved0, slot, sent, spread, ny, nz, cid):
     width = sent.shape[-1]
     dma = pltpu.SemaphoreType.DMA
     sems = exchange_sems(ny)
@@ -481,17 +527,27 @@
             jax.ShapeDtypeStruct((2, nz, NX, PA, NB), jnp.bfloat16),
             jax.ShapeDtypeStruct((2, NX, nz * PB, LANES), jnp.bfloat16),
             jax.ShapeDtypeStruct((2, NX, HALF, LANES), jnp.bfloat16),
-            jax.ShapeDtypeStruct((ny * CORES, 2, CAP // 2, width), jnp.bfloat16),
             jax.ShapeDtypeStruct((CORES, DCAP, width), jnp.bfloat16),
+            jax.ShapeDtypeStruct((2 * NB, 2 * width), jnp.bfloat16),
         ),
-        in_specs=[ANY] * 4,
-        out_specs=(ANY,) * 5,
-        scratch_shapes=sems
+        in_specs=[ANY] * 6,
+        out_specs=(ANY,) * 4 + (pl.BlockSpec(memory_space=pltpu.VMEM),),
+        scratch_shapes=[
+            pltpu.VMEM((ny * CORES, 2, CAP // 2, width), jnp.bfloat16),
+            pltpu.VMEM(rows0.shape, jnp.bfloat16),
+            pltpu.VMEM(moved0.shape, jnp.bfloat16),
+            pltpu.VMEM(slot.shape, jnp.int32),
+            pltpu.VMEM((NX, nz * PB, LANES), jnp.bfloat16),
+            pltpu.VMEM((NX, nz * PB, LANES), jnp.bfloat16),
+            dma((3,)),
+            dma,
+        ]
+        + sems
         + [zring, zring, zdirect, zdirect, xring, xring]
         + [dma((nz * NX,)), dma((2,)), xring, xring, dma((2,)), dma((2,)), dma((2,))],
         compiler_params=pltpu.CompilerParams(collective_id=cid, has_side_effects=True),
         name="second_exchange",
-    )(line, small, sent, spread)
+    )(line, rows0, moved0, slot, sent, spread)
 
 
 def dot(a, b):
@@ -630,53 +686,24 @@
     )(pivots, tile)
 
 
-def panel_tops_kernel(rows, moved, slot, small):
-    pcol, prow = lax.axis_index("pcol"), lax.axis_index("prow")
-    first = jnp.where(pcol == 0, NB, 0) + lax.rem(prow, CORES) * HALF
-    first = pl.multiple_of(first, HALF)
-    keys = slot[pl.ds(first, HALF), :]
-    total = rows.shape[0]
-    place = jnp.where(keys == lax.broadcasted_iota(jnp.int32, (HALF, total), 1), 1.0, 0.0).astype(jnp.bfloat16)
-    part = bdot(place, rows[...])
-    last = small.shape[1] - HALF - MOVED
-    for x in range(NX):
-        lanes = slice(x * LANES, (x + 1) * LANES)
-        small[x, pl.ds(0, HALF), :] = part[:, lanes]
-        small[x, pl.ds(HALF, MOVED), :] = moved[:, lanes]
-        small[x, pl.ds(HALF + MOVED, last), :] = jnp.zeros((last, LANES), jnp.bfloat16)
-
-
-def panel_tops(rows, moved, slot, nz):
-    vmem = pl.BlockSpec(memory_space=pltpu.VMEM)
-    return pl.pallas_call(
-        panel_tops_kernel,
-        out_shape=jax.ShapeDtypeStruct((NX, nz * PB, LANES), jnp.bfloat16),
-        in_specs=[vmem] * 3,
-        out_specs=vmem,
-        name="panel_tops",
-    )(rows, moved, slot)
-
-
-def update_kernel(raw, extra, other, rows0, rows1, moved0, moved1, slot, into, tile, low_inv, up_inv,
-                  out, top, low, up0, up1):
+def update_kernel(into, *refs):
+    sources, out, held = refs[:9], refs[9], refs[10:19]
+    low, up0, up1, sem = refs[19:]
+    fetches = [pltpu.make_async_copy(src, dst, sem.at[k]) for k, (src, dst) in enumerate(zip(sources, held))]
+    for copy in fetches:
+        copy.start()
+    low_inv, up_inv, top, extra, other, moved0, moved1, raw, tile = held
     pcol, prow = lax.axis_index("pcol"), lax.axis_index("prow")
     core = lax.rem(prow, CORES)
     f32 = jnp.float32
     step = NB // 2
     halves = (pl.ds(0, NB), pl.ds(NB, NB))
-    total = rows0.shape[0]
 
     def spot(i):
         return pl.ds(pl.multiple_of(i * step, step), step)
 
-    def place_rows(i, _):
-        keys = slot[spot(i), :]
-        place = jnp.where(keys == lax.broadcasted_iota(jnp.int32, (step, total), 1), 1.0, 0.0).astype(jnp.bfloat16)
-        top[spot(i), halves[0]] = bdot(place, rows0[...])
-        top[spot(i), halves[1]] = bdot(place, rows1[...])
-        return 0
-
-    lax.fori_loop(0, 4, place_rows, 0)
+    for copy in fetches[:5]:
+        copy.wait()
     l0, l1, u0, u1 = low_inv[0], low_inv[1], up_inv[0], up_inv[1]
     panel_tops = []
     for k in (0, 1):
@@ -693,6 +720,8 @@
         up0[:, cols] = bdot(l0, top[pl.ds(0, NB), cols])
         low[:, cols] = (top[pl.ds(NB, NB), cols].astype(f32) - dot(corner, up0[:, cols])).astype(jnp.bfloat16)
         up1[:, cols] = bdot(l1, low[:, cols])
+    for copy in fetches[5:]:
+        copy.wait()
 
     def update(i, _):
         here = spot(i)
@@ -731,18 +760,19 @@
         out[heads, halves[1]] = up1[:, halves[1]]
 
 
-def update(*args):
+def update(into, *args):
     n = 2 * NB
     vmem = pl.BlockSpec(memory_space=pltpu.VMEM)
     bf16 = jnp.bfloat16
     return pl.pallas_call(
         update_kernel,
         out_shape=jax.ShapeDtypeStruct((n, n), bf16),
-        in_specs=[vmem] * len(args),
+        in_specs=[vmem] + [ANY] * len(args),
         out_specs=vmem,
-        scratch_shapes=[pltpu.VMEM((n, n), bf16)] + [pltpu.VMEM((NB, n), bf16)] * 3,
+        scratch_shapes=[pltpu.VMEM(a.shape, bf16) for a in args]
+        + [pltpu.VMEM((NB, n), bf16)] * 3 + [pltpu.SemaphoreType.DMA((len(args),))],
         name="update",
-    )(*args)
+    )(into, *args)
 
 
 def count_before(flags):
@@ -852,24 +882,23 @@
         line, rows0, moved0 = first_exchange(tile, sents[0], spreads[0], ny, nz, cids[0])
         rows0, moved0 = rows0.reshape(nprow * CAP, NB), moved0.reshape(MOVED, NB)
         if known is not None:
-            rows0, moved0 = known[0], jnp.zeros_like(moved0)
-        small = panel_tops(rows0, moved0, slot, nz)
-        raw, extra, other, rows1, moved1 = second_exchange(line, small, sents[1], spreads[1], ny, nz, cids[1])
-        rows1, moved1 = rows1.reshape(nprow * CAP, NB), moved1.reshape(MOVED, NB)
+            rows0, moved0 = jnp.pad(known[:, :NB], ((0, nprow * CAP - n), (0, 0))), jnp.zeros_like(moved0)
+        raw, extra, other, moved1, top = second_exchange(
+            line, rows0, moved0, slot, sents[1], spreads[1], ny, nz, cids[1])
+        moved1 = moved1.reshape(MOVED, NB)
         if known is not None:
-            rows1, moved1 = known[1], jnp.zeros_like(moved1)
+            moved1, top = jnp.zeros_like(moved1), known
         return update(
-            raw.reshape(2, n, NB), extra, other, rows0, rows1, moved0, moved1, slot, into, tile, lower_inverse, upper_inverse)
+            into, lower_inverse, upper_inverse, top, extra, other, moved0, moved1, raw.reshape(2, n, NB), tile)
 
     def one_round(tile):
         return finish(tile, packed, slot, into, None, (0, 2))
 
     def many_rounds(tile):
         top, now = collect_rounds(tile, pivots, nprow, ny)
-        top = jnp.pad(top, ((0, nprow * CAP - n), (0, 0)))
         empty = [jnp.zeros_like(v) for v in packed]
         order = jnp.arange(n, dtype=jnp.int32)[:, None]
-        return finish(now, empty, order, jnp.full_like(into, -1), (top[:, :NB], top[:, NB:]), (3, 4))
+        return finish(now, empty, order, jnp.full_like(into, -1), top, (3, 4))
 
     out = lax.cond(rounds[0, 0] > 1, many_rounds, one_round, tile)
     return out.reshape(matrix.shape)

time: 110 us -> 107 us (0.973)
  Pallas kernels: 102 us -> 98.8 us
    pallas_call x1, Pallas kernels: 17.9 us -> 12.7 us  [update(): pl.pallas_call(update_kernel, out_shape=jax.ShapeDtypeStruct((n, n), bf16...]
    pallas_call x1, Pallas kernels: 36.1 us -> 40.9 us  [second_exchange(): pl.pallas_call(lambda *refs: second_kernel(ny, nz, len(sems), *refs), out...]
    pallas_call x1 -> x0, Pallas kernels: 2.96 us -> none  [panel_tops(): pl.pallas_call(panel_tops_kernel, out_shape=jax.ShapeDtypeStruct((NX, nz...]
where the time goes in v4:
time: 107 us
  Pallas kernels  98.8 us (92%)
  local copies, waits for them, and re-layouts  6.65 us (6%)
    pallas_call x1, Pallas kernels, second_exchange(): pl.pallas_call(lambda *refs: second_kernel(ny, nz, len(sems), *refs), out...  40.9 us
    pallas_call x1, Pallas kernels, first_exchange(): pl.pallas_call(lambda *refs: first_kernel(ny, nz, len(sems), *refs), out_...  35.9 us
    pallas_call x1, Pallas kernels, update(): pl.pallas_call(update_kernel, out_shape=jax.ShapeDtypeStruct((n, n), bf16...  12.7 us
    pallas_call x1, Pallas kernels, index_and_pack(): pl.pallas_call(lambda *refs: index_kernel(nprow, *refs), out_shape=(jax.S...  9.29 us
    reshape x1, local copies, waits for them, and re-layouts, per_device(): return out.reshape(matrix.shape)  4.48 us
    unnamed x5, local copies, waits for them, and re-layouts  2.17 us

profile of v4, /device:TPU:1, one launch (start us, length us, event | category | flops | bytes accessed | tf_op | source)
XLA Modules:
  0.0 106.7 jit_solution(12985290041268714895)
XLA Ops:
  0.0 0.0 copy-start.2
  0.0 2.2 %copy.9 = bf16[128,8,2,512]{3,1,2,0:T(8,128)(2,1)S(1)} copy(bf16[128,8,2,512]{3,2,1,0:T(2,128)(2,1)} %bitcast.49) | data formatting | bytes 4194304
  2.2 0.0 copy-start.1
  2.2 0.0 copy-done.2
  2.2 9.3 %index_and_pack.1 = (bf16[96,512]{1,0:T(8,128)(2,1)S(1)}, bf16[96,512]{1,0:T(8,128)(2,1)S(1)}, bf16[896,512]{1,0:T(8,128)(2,1)}, bf16[896,512]{1,0:T(8,128)(2,1)...) custom-call(s32[2,512]{1,0:T(2,128)S(1)} %copy-done.2, bf16[1024,1024]{1,0:T(8,128)(2,1)S(1)} %bitcast.43), custom_call_target="tpu_custom_call" | custom-call | tf_op jit(solution)/shard_map/index_and_pack/pallas_call | solution.py:675
  12.1 0.0 copy-done.1
  12.2 90.0 %conditional.1 = (bf16[1024,1024]{1,0:T(8,128)(2,1)}) conditional(s32[]{:T(128)} %bitcast.20, (bf16[96,512]{1,0:T(8,128)(2,1)S(1)}, bf16[896,512]{1,0:T(8,128)(2,1)}, bf16[1024,1024]{1,0:T(8,128)(2,1)S(1)}, bf16[96,512]{1,0:T(8,128)(2,1)S(1)}, bf16[896,512]{1,0:T(8,128)(2,1)}, /*index=5*/s32[1024,1]{1,0:T(8,128)}, s32[1,128]{1,0:T(1,128)S(1)}, ...), branch_computations={%region_0.0_spmd, %region_1.25_spmd} | conditional | flops 4629360128 | bytes 50367068 | solution.py:903
  12.2 35.9 %first_exchange.2 = (bf16[2,4,32,512]{3,2,1,0:T(8,128)(2,1)}, bf16[16,2,48,512]{3,2,1,0:T(8,128)(2,1)}, bf16[2,56,512]{2,1,0:T(8,128)(2,1)}) custom-call(bf16[1024,1024]{1,0:T(8,128)(2,1)S(1)} %get-tuple-element.305.refs_0_.refs_8_, bf16[2,48,512]{2,1,0:T(8,128)(2,1)S(1)} %bitcast.68, bf16[16,56,512]{2,1,0:T(8,128)(2,1)} %bitcast.53), custom_call_target="tpu_custom_call" | custom-call | tf_op jit(solution)/shard_map/cond/branch_0_fun/first_exchange/pallas_call | solution.py:380
  48.1 40.9 %second_exchange.2 = (bf16[2,8,4,32,512]{4,3,2,1,0:T(8,128)(2,1)}, bf16[2,4,384,128]{3,2,1,0:T(8,128)(2,1)}, bf16[2,4,256,128]{3,2,1,0:T(8,128)(2,1)}, bf16[2,56,512]{2,1,0:T(8,128)(2,1)}, bf16[1024,1024]{1,0:T(8,128)(2,1)}) custom-call(bf16[2,4,32,512]{3,2,1,0:T(8,128)(2,1)} %get-tuple-element.308.refs_0_, bf16[1536,512]{1,0:T(8,128)(2,1)} %bitcast.52, ...), custom_call_target="tpu_custom_call" | custom-call | tf_op jit(solution)/shard_map/cond/branch_0_fun/second_exchange/pallas_call | solution.py:524
  89.0 12.7 %update.2 = bf16[1024,1024]{1,0:T(8,128)(2,1)} custom-call(s32[1,128]{1,0:T(1,128)S(1)} %get-tuple-element.302.into, bf16[2,512,512]{2,1,0:T(8,128)(2,1)S(1)} %get-tuple-element.303.refs_0_, bf16[2,512,512]{2,1,0:T(8,128)(2,1)} %get-tuple-element.304.refs_1_, bf16[1024,1024]{1,0:T(8,128)(2,1)} %get-tuple-element.314.refs_2_, ...), custom_call_target="tpu_custom_call" | custom-call | tf_op jit(solution)/shard_map/cond/branch_0_fun/update/pallas_call | solution.py:767
  102.2 4.5 %reshape.383 = bf16[2,1,512,2,1,512]{5,3,2,0,4,1:T(2,128)(2,1)} reshape(bf16[1024,1024]{1,0:T(8,128)(2,1)} %get-tuple-element.369) | data formatting | bytes 4194304 | tf_op jit(solution)/shard_map/reshape | solution.py:904
Async XLA Ops:
  0.0 2.2 %copy-start.2 = (s32[2,512]{1,0:T(2,128)S(1)}, s32[2,512]{1,0:T(2,128)}, u32[]{:S(2)}) copy-start(s32[2,512]{1,0:T(2,128)} %refs_0_.1) | copy-start | bytes 12292
  2.2 10.0 %copy-start.1 = (bf16[2,512,512]{2,1,0:T(8,128)(2,1)S(1)}, bf16[2,512,512]{2,1,0:T(8,128)(2,1)}, u32[]{:S(2)}) copy-start(bf16[2,512,512]{2,1,0:T(8,128)(2,1)} %param.10) | copy-start | bytes 3145732

commit v5 on v4

--- a/solution.py
+++ b/solution.py
@@ -16,12 +16,14 @@
 PA = 32
 PB = 48
 MESH = pl.DeviceIdType.MESH
-T_Y, T_A0, T_A1, T_AD, T_BZ, T_BX, T_BXD, T_TOP = 4.5, 0.0, 2.5, 5.8, 3.5, 11.0, 4.0, 20.5
+T_Y, T_A0, T_A1, T_AD, T_BZ, T_BX, T_BXD, T_TOP, T_PLACE = 4.5, 0.0, 2.5, 5.8, 3.5, 11.0, 4.0, 20.5, 0.3
+T_PASS, T_LINE = 13.0, 16.5
 ANY = pl.BlockSpec(memory_space=pl.ANY)
 
 
 class Ring:
-    def __init__(self, n, pos, goto, item, send, recv, fresh=None, arrived=None):
+    def __init__(self, n, pos, goto, item, send, recv, fresh=None, arrived=None, first=1):
+        self.first = first
         self.n, self.pos, self.goto, self.item = n, pos, goto, item
         self.send, self.recv = send, recv
         self.fresh, self.arrived = fresh, arrived
@@ -35,8 +37,8 @@
         index = lax.rem(self.pos + self.n - step * (hop - 1), self.n)
         target = lax.rem(self.pos + self.n + step, self.n)
         src = self.item(index, half)
-        if hop == 1 and self.fresh is not None:
-            src = self.fresh(half)
+        if hop == self.first and self.fresh is not None:
+            src = self.fresh(way, half)
         return pltpu.make_async_remote_copy(
             src_ref=src,
             dst_ref=self.item(index, half),
@@ -61,7 +63,7 @@
 
     def start(self, half):
         for way in (0, 1):
-            self.copy(way, 1, half).start()
+            self.copy(way, self.first, half).start()
 
     def step(self, way, hop, half):
         index, ref, arrival = self.landed(way, hop, half)
@@ -75,19 +77,19 @@
     def events(self, t0, dt):
         out = []
         for half in (0, 1):
-            for hop in range(1, self.n // 2 + 1):
+            for hop in range(self.first, self.n // 2 + 1):
                 for way in (0, 1):
                     if self.carries(way, hop, half):
-                        when = t0[half] + dt * hop
+                        when = t0[half] + dt * (hop - self.first + 1)
                         out.append((when, lambda w=way, h=hop, f=half: self.step(w, h, f)))
         return out
 
     def complete(self, half):
-        assert self.got[half] == self.n - 1
+        assert self.got[half] == self.n + 1 - 2 * self.first
 
     def drain(self):
         for half in (0, 1):
-            for hop in range(1, self.n // 2 + 1):
+            for hop in range(self.first, self.n // 2 + 1):
                 for way in (0, 1):
                     if self.carries(way, hop, half):
                         self.copy(way, hop, half).wait_send()
@@ -110,7 +112,7 @@
             lambda i: {"prow": i * CORES + self.c},
             lambda i, half: rows.at[i * CORES + self.c, half],
             self.rs, self.rr,
-            fresh=lambda half: sent.at[half],
+            fresh=lambda way, half: sent.at[half],
             arrived=self.forward,
         )
         self.forwards = []
@@ -346,9 +348,9 @@
 
 
 def first_kernel(ny, nz, nexch, *refs):
-    tile, sent, spread, line, rows, moved = refs[:6]
-    ex = RowExchange(ny, sent, spread, rows, moved, refs[6 : 6 + nexch])
-    ss, sr, xs, xr = refs[6 + nexch :]
+    tile, sent, spread, line, beside, rows, moved = refs[:7]
+    ex = RowExchange(ny, sent, spread, rows, moved, refs[7 : 7 + nexch])
+    ss, sr, xs, xr, zs, zr = refs[7 + nexch :]
     pcol = lax.axis_index("pcol")
     n = nz * NX
     z, x = lax.div(pcol, NX), lax.rem(pcol, NX)
@@ -358,6 +360,21 @@
         lambda panel, to: line.at[panel, lax.rem(to, NX)], ss, sr)
     gather = Direct(NX, x, lambda i: {"pcol": z * NX + i}, lambda i, h: line.at[h, i], xs, xr)
     near = ex.barrier_peers() + [{"pcol": z * NX + lax.rem(x + d, NX)} for d in range(1, NX)]
+    around = [{"pcol": lax.rem(z + d, nz) * NX + x} for d in (1, nz - 1)]
+    near += around
+
+    def next_line(way, half):
+        return pltpu.make_async_remote_copy(
+            src_ref=line.at[half], dst_ref=beside.at[way, half],
+            send_sem=zs.at[way, half], recv_sem=zr.at[way, half],
+            device_id=around[way], device_id_type=MESH)
+
+    def send_lines():
+        for half in (0, 1):
+            gather.wait(half)
+            for way in (0, 1):
+                next_line(way, half).start()
+
     meet_with_roots(near, pcol, n)
 
     def pass_on():
@@ -365,10 +382,11 @@
             scatter.landed(panel)
             gather.start_half(panel)
 
-    run_events(ex.events(3.8) + [(-0.5, scatter.start), (13.0, pass_on)])
+    run_events(ex.events(3.8) + [(-0.5, scatter.start), (T_PASS, pass_on), (T_LINE, send_lines)])
     ex.finish()
-    for panel in (0, 1):
-        gather.wait(panel)
+    for half in (0, 1):
+        for way in (0, 1):
+            next_line(way, half).wait()
     gather.drain()
     scatter.drain()
 
@@ -381,22 +399,24 @@
         lambda *refs: first_kernel(ny, nz, len(sems), *refs),
         out_shape=(
             jax.ShapeDtypeStruct((2, NX, PA, NB), jnp.bfloat16),
+            jax.ShapeDtypeStruct((2, 2, NX, PA, NB), jnp.bfloat16),
             jax.ShapeDtypeStruct((ny * CORES, 2, CAP // 2, width), jnp.bfloat16),
             jax.ShapeDtypeStruct((CORES, DCAP, width), jnp.bfloat16),
         ),
         in_specs=[ANY] * 3,
-        out_specs=(ANY,) * 3,
-        scratch_shapes=sems + [dma((nz * NX,)), dma((2,)), dma((NX, 2)), dma((NX, 2))],
+        out_specs=(ANY,) * 4,
+        scratch_shapes=sems
+        + [dma((nz * NX,)), dma((2,)), dma((NX, 2)), dma((NX, 2)), dma((2, 2)), dma((2, 2))],
         compiler_params=pltpu.CompilerParams(collective_id=cid, has_side_effects=True),
         name="first_exchange",
     )(tile, sent, spread)
 
 
 def second_kernel(ny, nz, nexch, *refs):
-    line, rows_first, moved_first, slot_in, sent, spread, raw, extra, other, moved, top = refs[:11]
+    beside, rows_first, moved_first, slot_in, sent, spread, raw, extra, other, moved, top = refs[:11]
     rows, rows0, moved0, slot, made, small, fetch_sem, small_sem = refs[11:19]
     ex = RowExchange(ny, sent, spread, rows, moved, refs[19 : 19 + nexch])
-    (azs, azr, bzs, bzr, bxs, bxr, ss, sr, ts, tr, to_s, to_r, own) = refs[19 + nexch :]
+    (azs, azr, bzs, bzr, bxs, bxr, ss, sr, ts, tr, to_s, to_r) = refs[19 + nexch :]
     total = rows0.shape[0]
     pcol = lax.axis_index("pcol")
     n = nz * NX
@@ -443,7 +463,6 @@
             made[k, pl.ds(0, HALF), :] = part[:, lanes]
             made[k, pl.ds(HALF, MOVED), :] = moved0[:, lanes]
             made[k, pl.ds(HALF + MOVED, last), :] = jnp.zeros((last, LANES), jnp.bfloat16)
-        place_rows(lambda: rows0[...], pl.ds(0, NB))
         handover = pltpu.make_async_copy(made, small, small_sem)
         handover.start()
         handover.wait()
@@ -470,16 +489,16 @@
         pcol, n,
         lambda to: small.at[lax.rem(to, NX), band(lax.div(to, NX))],
         lambda panel, to: extra.at[panel, lax.rem(to, NX), band(lax.div(to, NX))], ss, sr)
-    az = Ring(nz, z, to_z, lambda i, h: raw.at[h, i], azs, azr, fresh=lambda h: line.at[h])
+    az = Ring(nz, z, to_z, lambda i, h: raw.at[h, i], azs, azr,
+              fresh=lambda way, h: beside.at[way, h], first=2)
     bz = Direct(nz, z, to_z, lambda i, h: extra.at[h, x, band(i)], bzs, bzr)
     bx = Ring(NX, x, to_x, lambda i, h: extra.at[h, i], bxs, bxr, arrived=cross)
-    keep = [pltpu.make_async_copy(line.at[h], raw.at[h, z], own.at[h]) for h in (0, 1)]
 
     def begin_az():
         for half in (0, 1):
-            az.start(half)
-        for copy in keep:
-            copy.start()
+            for way in (0, 1):
+                if az.carries(way, 2, half):
+                    az.copy(way, 2, half).start()
 
     def begin_bz():
         for half in (0, 1):
@@ -502,7 +521,7 @@
         ex.finish()
         place_rows(lambda: rows[...].reshape(total, NB), pl.ds(NB, NB))
 
-    events += [(T_TOP, last_rows)]
+    events += [(T_TOP, last_rows), (T_PLACE, lambda: place_rows(lambda: rows0[...], pl.ds(0, NB)))]
     run_events(events)
     for ring in (az, bx):
         for half in (0, 1):
@@ -512,11 +531,9 @@
     scatter.drain()
     for copy in crossing:
         copy.wait()
-    for copy in keep:
-        copy.wait()
-
-
-def second_exchange(line, rows0, moved0, slot, sent, spread, ny, nz, cid):
+
+
+def second_exchange(beside, rows0, moved0, slot, sent, spread, ny, nz, cid):
     width = sent.shape[-1]
     dma = pltpu.SemaphoreType.DMA
     sems = exchange_sems(ny)
@@ -544,10 +561,10 @@
         ]
         + sems
         + [zring, zring, zdirect, zdirect, xring, xring]
-        + [dma((nz * NX,)), dma((2,)), xring, xring, dma((2,)), dma((2,)), dma((2,))],
+        + [dma((nz * NX,)), dma((2,)), xring, xring, dma((2,)), dma((2,))],
         compiler_params=pltpu.CompilerParams(collective_id=cid, has_side_effects=True),
         name="second_exchange",
-    )(line, rows0, moved0, slot, sent, spread)
+    )(beside, rows0, moved0, slot, sent, spread)
 
 
 def dot(a, b):
@@ -687,12 +704,19 @@
 
 
 def update_kernel(into, *refs):
-    sources, out, held = refs[:9], refs[9], refs[10:19]
-    low, up0, up1, sem = refs[19:]
-    fetches = [pltpu.make_async_copy(src, dst, sem.at[k]) for k, (src, dst) in enumerate(zip(sources, held))]
+    sources, (raw_in, line, beside), out, held, raw = refs[:8], refs[8:11], refs[11], refs[12:20], refs[20]
+    low, up0, up1, sem = refs[21:]
+    nz = raw.shape[1]
+    z = lax.div(lax.axis_index("pcol"), NX)
+    pairs = list(zip(sources, held))
+    for k in range(nz):
+        at = lax.rem(z + k, nz)
+        src = line if k == 0 else beside.at[1] if k == 1 else beside.at[0] if k == nz - 1 else raw_in.at[:, at]
+        pairs.append((src, raw.at[:, at]))
+    fetches = [pltpu.make_async_copy(src, dst, sem.at[k]) for k, (src, dst) in enumerate(pairs)]
     for copy in fetches:
         copy.start()
-    low_inv, up_inv, top, extra, other, moved0, moved1, raw, tile = held
+    low_inv, up_inv, top, extra, other, moved0, moved1, tile = held
     pcol, prow = lax.axis_index("pcol"), lax.axis_index("prow")
     core = lax.rem(prow, CORES)
     f32 = jnp.float32
@@ -730,11 +754,13 @@
         hit = jnp.max(match, axis=1, keepdims=True) > 0.5
         insert = match.astype(jnp.bfloat16)
 
+        lines = pl.ds(i * (step // raw.shape[2]), step // raw.shape[2])
+
         def with_moved(new, old):
             return jnp.where(hit, dot(insert, new), old.astype(f32)).astype(jnp.bfloat16)
 
-        factor0 = bdot(with_moved(moved_panel[0], raw[0, here, :]), u0)
-        panel1 = (with_moved(moved_panel[1], raw[1, here, :]).astype(f32) - dot(factor0, upper)).astype(jnp.bfloat16)
+        factor0 = bdot(with_moved(moved_panel[0], raw[0, lines].reshape(step, NB)), u0)
+        panel1 = (with_moved(moved_panel[1], raw[1, lines].reshape(step, NB)).astype(f32) - dot(factor0, upper)).astype(jnp.bfloat16)
         factor1 = bdot(panel1, u1)
         for d, (cols, moved) in enumerate(zip(halves, (moved0, moved1))):
             new = with_moved(moved[...], tile[here, cols]).astype(f32)
@@ -764,13 +790,14 @@
     n = 2 * NB
     vmem = pl.BlockSpec(memory_space=pltpu.VMEM)
     bf16 = jnp.bfloat16
+    held = [pltpu.VMEM(a.shape, bf16) for a in args[:9]]
     return pl.pallas_call(
         update_kernel,
         out_shape=jax.ShapeDtypeStruct((n, n), bf16),
         in_specs=[vmem] + [ANY] * len(args),
         out_specs=vmem,
-        scratch_shapes=[pltpu.VMEM(a.shape, bf16) for a in args]
-        + [pltpu.VMEM((NB, n), bf16)] * 3 + [pltpu.SemaphoreType.DMA((len(args),))],
+        scratch_shapes=held
+        + [pltpu.VMEM((NB, n), bf16)] * 3 + [pltpu.SemaphoreType.DMA((8 + args[8].shape[1],))],
         name="update",
     )(into, *args)
 
@@ -879,17 +906,18 @@
     def finish(tile, packed, slot, into, known, cids):
         sents = [v.reshape(2, CAP // 2, NB) for v in packed[:2]]
         spreads = [v.reshape(nprow, DCAP, NB) for v in packed[2:]]
-        line, rows0, moved0 = first_exchange(tile, sents[0], spreads[0], ny, nz, cids[0])
+        line, beside, rows0, moved0 = first_exchange(tile, sents[0], spreads[0], ny, nz, cids[0])
         rows0, moved0 = rows0.reshape(nprow * CAP, NB), moved0.reshape(MOVED, NB)
         if known is not None:
             rows0, moved0 = jnp.pad(known[:, :NB], ((0, nprow * CAP - n), (0, 0))), jnp.zeros_like(moved0)
         raw, extra, other, moved1, top = second_exchange(
-            line, rows0, moved0, slot, sents[1], spreads[1], ny, nz, cids[1])
+            beside, rows0, moved0, slot, sents[1], spreads[1], ny, nz, cids[1])
         moved1 = moved1.reshape(MOVED, NB)
         if known is not None:
             moved1, top = jnp.zeros_like(moved1), known
         return update(
-            into, lower_inverse, upper_inverse, top, extra, other, moved0, moved1, raw.reshape(2, n, NB), tile)
+            into, lower_inverse, upper_inverse, top, extra, other, moved0, moved1, tile,
+            raw.reshape(2, nz, NX * PA, NB), line.reshape(2, NX * PA, NB), beside.reshape(2, 2, NX * PA, NB))
 
     def one_round(tile):
         return finish(tile, packed, slot, into, None, (0, 2))

time: 107 us -> 107 us (level)
    pallas_call x1, Pallas kernels: 35.9 us -> 37.2 us  [first_exchange(): pl.pallas_call(lambda *refs: first_kernel(ny, nz, len(sems), *refs), out_...]
where the time goes in v5:
time: 107 us
  Pallas kernels  99.2 us (93%)
  local copies, waits for them, and re-layouts  6.65 us (6%)
    pallas_call x1, Pallas kernels, second_exchange(): pl.pallas_call(lambda *refs: second_kernel(ny, nz, len(sems), *refs), out...  39.9 us
    pallas_call x1, Pallas kernels, first_exchange(): pl.pallas_call(lambda *refs: first_kernel(ny, nz, len(sems), *refs), out_...  37.2 us
    pallas_call x1, Pallas kernels, update(): pl.pallas_call(update_kernel, out_shape=jax.ShapeDtypeStruct((n, n), bf16...  12.8 us
    pallas_call x1, Pallas kernels, index_and_pack(): pl.pallas_call(lambda *refs: index_kernel(nprow, *refs), out_shape=(jax.S...  9.29 us
    reshape x1, local copies, waits for them, and re-layouts, per_device(): return out.reshape(matrix.shape)  4.48 us
    unnamed x5, local copies, waits for them, and re-layouts  2.17 us

profile of v5, /device:TPU:1, one launch (start us, length us, event | category | flops | bytes accessed | tf_op | source)
XLA Modules:
  0.0 107.1 jit_solution(16625583061223398563)
XLA Ops:
  0.0 0.0 copy-start.2
  0.0 2.2 %copy.9 = bf16[128,8,2,512]{3,1,2,0:T(8,128)(2,1)S(1)} copy(bf16[128,8,2,512]{3,2,1,0:T(2,128)(2,1)} %bitcast.57) | data formatting | bytes 4194304
  2.2 0.0 copy-start.1
  2.2 0.0 copy-done.2
  2.2 9.3 %index_and_pack.1 = (bf16[96,512]{1,0:T(8,128)(2,1)S(1)}, bf16[96,512]{1,0:T(8,128)(2,1)S(1)}, bf16[896,512]{1,0:T(8,128)(2,1)}, bf16[896,512]{1,0:T(8,128)(2,1)...) custom-call(s32[2,512]{1,0:T(2,128)S(1)} %copy-done.2, bf16[1024,1024]{1,0:T(8,128)(2,1)S(1)} %bitcast.47), custom_call_target="tpu_custom_call" | custom-call | tf_op jit(solution)/shard_map/index_and_pack/pallas_call | solution.py:692
  12.1 0.0 copy-done.1
  12.2 90.4 %conditional.1 = (bf16[1024,1024]{1,0:T(8,128)(2,1)}) conditional(s32[]{:T(128)} %bitcast.24, (bf16[96,512]{1,0:T(8,128)(2,1)S(1)}, bf16[896,512]{1,0:T(8,128)(2,1)}, bf16[1024,1024]{1,0:T(8,128)(2,1)S(1)}, bf16[96,512]{1,0:T(8,128)(2,1)S(1)}, bf16[896,512]{1,0:T(8,128)(2,1)}, /*index=5*/s32[1024,1]{1,0:T(8,128)}, s32[1,128]{1,0:T(1,128)S(1)}, ...), branch_computations={%region_0.0_spmd, %region_1.25_spmd} | conditional | flops 4629360128 | bytes 50367068 | solution.py:931
  12.2 37.2 %first_exchange.2 = (bf16[2,4,32,512]{3,2,1,0:T(8,128)(2,1)}, bf16[2,2,4,32,512]{4,3,2,1,0:T(8,128)(2,1)}, bf16[16,2,48,512]{3,2,1,0:T(8,128)(2,1)}, bf16[2,56,512]{2,1,0:T(8,128)(2,1)}) custom-call(bf16[1024,1024]{1,0:T(8,128)(2,1)S(1)} %get-tuple-element.305.refs_0_.refs_7_, bf16[2,48,512]{2,1,0:T(8,128)(2,1)S(1)} %bitcast.76, bf16[16,56,512]{2,1,0:T(8,128)(2,1)} %bitcast.60), custom_call_target="tpu_custom_call" | custom-call | tf_op jit(solution)/shard_map/cond/branch_0_fun/first_exchange/pallas_call | solution.py:398
  49.4 39.9 %second_exchange.2 = (bf16[2,8,4,32,512]{4,3,2,1,0:T(8,128)(2,1)}, bf16[2,4,384,128]{3,2,1,0:T(8,128)(2,1)}, bf16[2,4,256,128]{3,2,1,0:T(8,128)(2,1)}, bf16[2,56,512]{2,1,0:T(8,128)(2,1)}, bf16[1024,1024]{1,0:T(8,128)(2,1)}) custom-call(bf16[2,2,4,32,512]{4,3,2,1,0:T(8,128)(2,1)} %get-tuple-element.308.refs_0_, bf16[1536,512]{1,0:T(8,128)(2,1)} %bitcast.58, ...), custom_call_target="tpu_custom_call" | custom-call | tf_op jit(solution)/shard_map/cond/branch_0_fun/second_exchange/pallas_call | solution.py:541
  89.3 12.8 %update.2 = bf16[1024,1024]{1,0:T(8,128)(2,1)} custom-call(s32[1,128]{1,0:T(1,128)S(1)} %get-tuple-element.302.into, bf16[2,512,512]{2,1,0:T(8,128)(2,1)S(1)} %get-tuple-element.303.refs_0_, bf16[2,512,512]{2,1,0:T(8,128)(2,1)} %get-tuple-element.304.refs_1_, bf16[1024,1024]{1,0:T(8,128)(2,1)} %get-tuple-element.314.refs_2_, ...), custom_call_target="tpu_custom_call" | custom-call | tf_op jit(solution)/shard_map/cond/branch_0_fun/update/pallas_call | solution.py:794
  102.6 4.5 %reshape.395 = bf16[2,1,512,2,1,512]{5,3,2,0,4,1:T(2,128)(2,1)} reshape(bf16[1024,1024]{1,0:T(8,128)(2,1)} %get-tuple-element.371) | data formatting | bytes 4194304 | tf_op jit(solution)/shard_map/reshape | solution.py:932
Async XLA Ops:
  0.0 2.2 %copy-start.2 = (s32[2,512]{1,0:T(2,128)S(1)}, s32[2,512]{1,0:T(2,128)}, u32[]{:S(2)}) copy-start(s32[2,512]{1,0:T(2,128)} %refs_0_.1) | copy-start | bytes 12292
  2.2 10.0 %copy-start.1 = (bf16[2,512,512]{2,1,0:T(8,128)(2,1)S(1)}, bf16[2,512,512]{2,1,0:T(8,128)(2,1)}, u32[]{:S(2)}) copy-start(bf16[2,512,512]{2,1,0:T(8,128)(2,1)} %param.10) | copy-start | bytes 3145732

commit v6 on v5

--- a/solution.py
+++ b/solution.py
@@ -17,7 +17,7 @@
 PB = 48
 MESH = pl.DeviceIdType.MESH
 T_Y, T_A0, T_A1, T_AD, T_BZ, T_BX, T_BXD, T_TOP, T_PLACE = 4.5, 0.0, 2.5, 5.8, 3.5, 11.0, 4.0, 20.5, 0.3
-T_PASS, T_LINE = 13.0, 16.5
+T_PASS, T_LINE = 9.5, 12.8
 ANY = pl.BlockSpec(memory_space=pl.ANY)
 
 

time: 107 us -> 107 us (level)
    pallas_call x1, Pallas kernels: 37.2 us -> 36 us  [first_exchange(): pl.pallas_call(lambda *refs: first_kernel(ny, nz, len(sems), *refs), out_...]
where the time goes in v6:
time: 107 us; the launch traced here: 106 us
  Pallas kernels  98.3 us (92%)
  local copies, waits for them, and re-layouts  6.65 us (6%)
    pallas_call x1, Pallas kernels, second_exchange(): pl.pallas_call(lambda *refs: second_kernel(ny, nz, len(sems), *refs), out...  40.3 us
    pallas_call x1, Pallas kernels, first_exchange(): pl.pallas_call(lambda *refs: first_kernel(ny, nz, len(sems), *refs), out_...  36 us
    pallas_call x1, Pallas kernels, update(): pl.pallas_call(update_kernel, out_shape=jax.ShapeDtypeStruct((n, n), bf16...  12.8 us
    pallas_call x1, Pallas kernels, index_and_pack(): pl.pallas_call(lambda *refs: index_kernel(nprow, *refs), out_shape=(jax.S...  9.29 us
    reshape x1, local copies, waits for them, and re-layouts, per_device(): return out.reshape(matrix.shape)  4.48 us
    unnamed x5, local copies, waits for them, and re-layouts  2.17 us

profile of v6, /device:TPU:1, one launch (start us, length us, event | category | flops | bytes accessed | tf_op | source)
XLA Modules:
  0.0 106.2 jit_solution(15054609801090883556)
XLA Ops:
  0.0 0.0 copy-start.2
  0.0 2.2 %copy.9 = bf16[128,8,2,512]{3,1,2,0:T(8,128)(2,1)S(1)} copy(bf16[128,8,2,512]{3,2,1,0:T(2,128)(2,1)} %bitcast.57) | data formatting | bytes 4194304
  2.2 0.0 copy-start.1
  2.2 0.0 copy-done.2
  2.2 9.3 %index_and_pack.1 = (bf16[96,512]{1,0:T(8,128)(2,1)S(1)}, bf16[96,512]{1,0:T(8,128)(2,1)S(1)}, bf16[896,512]{1,0:T(8,128)(2,1)}, bf16[896,512]{1,0:T(8,128)(2,1)...) custom-call(s32[2,512]{1,0:T(2,128)S(1)} %copy-done.2, bf16[1024,1024]{1,0:T(8,128)(2,1)S(1)} %bitcast.47), custom_call_target="tpu_custom_call" | custom-call | tf_op jit(solution)/shard_map/index_and_pack/pallas_call | solution.py:692
  12.1 0.0 copy-done.1
  12.2 89.6 %conditional.1 = (bf16[1024,1024]{1,0:T(8,128)(2,1)}) conditional(s32[]{:T(128)} %bitcast.24, (bf16[96,512]{1,0:T(8,128)(2,1)S(1)}, bf16[896,512]{1,0:T(8,128)(2,1)}, bf16[1024,1024]{1,0:T(8,128)(2,1)S(1)}, bf16[96,512]{1,0:T(8,128)(2,1)S(1)}, bf16[896,512]{1,0:T(8,128)(2,1)}, /*index=5*/s32[1024,1]{1,0:T(8,128)}, s32[1,128]{1,0:T(1,128)S(1)}, ...), branch_computations={%region_0.0_spmd, %region_1.25_spmd} | conditional | flops 4629360128 | bytes 50367068 | solution.py:931
  12.2 36.0 %first_exchange.2 = (bf16[2,4,32,512]{3,2,1,0:T(8,128)(2,1)}, bf16[2,2,4,32,512]{4,3,2,1,0:T(8,128)(2,1)}, bf16[16,2,48,512]{3,2,1,0:T(8,128)(2,1)}, bf16[2,56,512]{2,1,0:T(8,128)(2,1)}) custom-call(bf16[1024,1024]{1,0:T(8,128)(2,1)S(1)} %get-tuple-element.305.refs_0_.refs_7_, bf16[2,48,512]{2,1,0:T(8,128)(2,1)S(1)} %bitcast.76, bf16[16,56,512]{2,1,0:T(8,128)(2,1)} %bitcast.60), custom_call_target="tpu_custom_call" | custom-call | tf_op jit(solution)/shard_map/cond/branch_0_fun/first_exchange/pallas_call | solution.py:398
  48.2 40.3 %second_exchange.2 = (bf16[2,8,4,32,512]{4,3,2,1,0:T(8,128)(2,1)}, bf16[2,4,384,128]{3,2,1,0:T(8,128)(2,1)}, bf16[2,4,256,128]{3,2,1,0:T(8,128)(2,1)}, bf16[2,56,512]{2,1,0:T(8,128)(2,1)}, bf16[1024,1024]{1,0:T(8,128)(2,1)}) custom-call(bf16[2,2,4,32,512]{4,3,2,1,0:T(8,128)(2,1)} %get-tuple-element.308.refs_0_, bf16[1536,512]{1,0:T(8,128)(2,1)} %bitcast.58, ...), custom_call_target="tpu_custom_call" | custom-call | tf_op jit(solution)/shard_map/cond/branch_0_fun/second_exchange/pallas_call | solution.py:541
  88.4 12.8 %update.2 = bf16[1024,1024]{1,0:T(8,128)(2,1)} custom-call(s32[1,128]{1,0:T(1,128)S(1)} %get-tuple-element.302.into, bf16[2,512,512]{2,1,0:T(8,128)(2,1)S(1)} %get-tuple-element.303.refs_0_, bf16[2,512,512]{2,1,0:T(8,128)(2,1)} %get-tuple-element.304.refs_1_, bf16[1024,1024]{1,0:T(8,128)(2,1)} %get-tuple-element.314.refs_2_, ...), custom_call_target="tpu_custom_call" | custom-call | tf_op jit(solution)/shard_map/cond/branch_0_fun/update/pallas_call | solution.py:794
  101.8 4.5 %reshape.395 = bf16[2,1,512,2,1,512]{5,3,2,0,4,1:T(2,128)(2,1)} reshape(bf16[1024,1024]{1,0:T(8,128)(2,1)} %get-tuple-element.371) | data formatting | bytes 4194304 | tf_op jit(solution)/shard_map/reshape | solution.py:932
Async XLA Ops:
  0.0 2.2 %copy-start.2 = (s32[2,512]{1,0:T(2,128)S(1)}, s32[2,512]{1,0:T(2,128)}, u32[]{:S(2)}) copy-start(s32[2,512]{1,0:T(2,128)} %refs_0_.1) | copy-start | bytes 12292
  2.2 10.0 %copy-start.1 = (bf16[2,512,512]{2,1,0:T(8,128)(2,1)S(1)}, bf16[2,512,512]{2,1,0:T(8,128)(2,1)}, u32[]{:S(2)}) copy-start(bf16[2,512,512]{2,1,0:T(8,128)(2,1)} %param.10) | copy-start | bytes 3145732
